TPU v7x, 32 devices: a whole 2x2x4 slice. The times are simulated.
32 devices in a mesh: ctx: 4 (over z), tp: 8 (over y, x, core).
Axes of the slice: x: 2, y: 2, z: 4, core: 2. Of those that a mesh axis runs over, the one named last changes fastest.
Arguments:
- stream: bfloat16 [2048, 4096], P('ctx'), may hold values from -6 to 6
- time_previous_token: bfloat16 [4096], replicated, may hold values from -6 to 6
- channel_previous_token: bfloat16 [4096], replicated, may hold values from -15 to 15
- head_state_initial: float32 [64, 64, 64], P('tp'), may hold values from -60 to 60
- time_norm_gain: float32 [4096], replicated, may hold values from 0.5 to 1.5
- time_norm_bias: float32 [4096], replicated, may hold values from -1.2 to 1.2
- time_shift_weights: bfloat16 [6, 4096], replicated, may hold values from 0 to 1
- receptance: bfloat16 [4096, 4096], P(None, 'tp'), may hold values from -0.09375 to 0.09375
- key_projection_matrix: bfloat16 [4096, 4096], P(None, 'tp'), may hold values from -0.09375 to 0.09375
- value_projection_matrix: bfloat16 [4096, 4096], P(None, 'tp'), may hold values from -0.09375 to 0.09375
- decay_first_factor: bfloat16 [4096, 128], replicated, may hold values from -0.09375 to 0.09375
- decay_second_factor: bfloat16 [128, 4096], P(None, 'tp'), may hold values from -1 to 1
- decay_channel_base: float32 [4096], P('tp'), may hold values from -12 to -2, as said below
- rate_first_factor: bfloat16 [4096, 128], replicated, may hold values from -0.09375 to 0.09375
- rate_second_factor: bfloat16 [128, 4096], P(None, 'tp'), may hold values from -0.5 to 0.5
- rate_channel_base: float32 [4096], P('tp'), may hold values from -1.5 to 1.5
- gate_first_factor: bfloat16 [4096, 256], replicated, may hold values from -0.09375 to 0.09375
- gate_second_factor: bfloat16 [256, 4096], P(None, 'tp'), may hold values from -0.375 to 0.375
- removal_key_scale: float32 [4096], P('tp'), may hold values from 0.5 to 1.5
- key_rate_scale: float32 [4096], P('tp'), may hold values from 0.1 to 0.7
- self_lookup_coefficient: float32 [4096], P('tp'), may hold values from -1.2 to 1.2
- head_group_gain: float32 [4096], P('tp'), may hold values from 0.5 to 1.5
- head_group_bias: float32 [4096], P('tp'), may hold values from -1.2 to 1.2
- time_output_weight: bfloat16 [4096, 4096], P('tp'), may hold values from -0.09375 to 0.09375
- channel_norm_gain: float32 [4096], replicated, may hold values from 0.5 to 1.5
- channel_norm_bias: float32 [4096], replicated, may hold values from -1.2 to 1.2
- channel_shift_weight: bfloat16 [4096], replicated, may hold values from 0 to 1
- channel_key_weight: bfloat16 [4096, 8192], P(None, 'tp'), may hold values from -0.09375 to 0.09375
- channel_value_weight: bfloat16 [8192, 4096], P('tp'), may hold values from -0.0625 to 0.0625
Outputs:
- layer_out: bfloat16 [2048, 4096], P('ctx')
Inputs may be any that keep to these rules, and one draw needn't show every extreme that they name: `decay_channel_base`: Channel-wise values of the decay's base.
All inputs are finite; a program needn't handle non-finite values.
Results may differ from a plain program's by a relative error of at most 0.018.
Values may be sent and summed in bfloat16 or wider, within the bound.
A program may use at most 192 MiB of HBM per device.

v0:
```python
import jax
import jax.numpy as jnp
from jax import lax
from jax.sharding import PartitionSpec as P

LANE_SPAN = 64
SPAN = 64


def passed_along(shard, axis, by):
    length = lax.axis_size(axis)
    pairs = [(i, i + by) for i in range(length) if 0 <= i + by < length]
    return lax.ppermute(shard, axis, pairs)


def layer_norm(matrix, gain_vec, bias_vec):
    floats = matrix.astype(jnp.float32)
    average = jnp.mean(floats, axis=-1, keepdims=True)
    centered = floats - average
    variance = jnp.mean(centered * centered, axis=-1, keepdims=True)
    return (centered * lax.rsqrt(variance + 1e-05) * gain_vec + bias_vec).astype(jnp.bfloat16)


def mixed_input(normed, previous, weight_vec):
    current = normed.astype(jnp.float32)
    return (
        current + (previous.astype(jnp.float32) - current) * weight_vec.astype(jnp.float32)
    ).astype(jnp.bfloat16)


def compose(left, right):
    return jnp.einsum("hij,hjk->hik", left, right, precision=lax.Precision.HIGHEST)


def pair_product(first, second, keep_mask):
    product = jnp.einsum("hctj,hcsj->hcts", first, second, precision=lax.Precision.HIGHEST)
    return jnp.where(keep_mask, product, 0.0)


def block_terms(recept_c, log_decay_c, norm_key_c, rate_c, key_adj_c, value_c):
    highest = lax.Precision.HIGHEST
    cumulative = jnp.cumsum(log_decay_c, axis=2)
    before = cumulative - log_decay_c
    total_log = cumulative[:, :, -1:, :]
    centre = 0.5 * total_log
    alpha = -norm_key_c
    beta = rate_c * norm_key_c
    left_side = alpha * jnp.exp(before - centre)
    recept_side = recept_c * jnp.exp(cumulative - centre)
    beta_side = beta * jnp.exp(centre - cumulative)
    key_side = key_adj_c * jnp.exp(centre - cumulative)
    length = recept_c.shape[2]
    size_head = recept_c.shape[3]
    lower_index = lax.broadcasted_iota(jnp.int32, (length, length), 0)
    upper_index = lax.broadcasted_iota(jnp.int32, (length, length), 1)
    strict = lower_index > upper_index
    inclusive = lower_index >= upper_index
    rate_pairs = pair_product(left_side, beta_side, strict)
    key_pairs = pair_product(left_side, key_side, strict)
    read_rate = pair_product(recept_side, beta_side, inclusive)
    read_key = pair_product(recept_side, key_side, inclusive)
    system = jnp.eye(length, dtype=jnp.float32) - rate_pairs
    driven = jnp.einsum("hcts,hcsi->hcti", key_pairs, value_c, precision=highest)
    right_hand = jnp.concatenate([driven, alpha * jnp.exp(before)], axis=-1)
    solved = jax.scipy.linalg.solve_triangular(system, right_hand, lower=True, unit_diagonal=True)
    removal = solved[..., :size_head]
    carried = solved[..., size_head:]
    zero_out = jnp.einsum("hcts,hcsi->hcti", read_rate, removal, precision=highest) + jnp.einsum(
        "hcts,hcsi->hcti", read_key, value_c, precision=highest
    )
    reader = recept_c * jnp.exp(cumulative) + jnp.einsum(
        "hcts,hcsj->hctj", read_rate, carried, precision=highest
    )
    beta_end = beta * jnp.exp(total_log - cumulative)
    key_end = key_adj_c * jnp.exp(total_log - cumulative)
    transfer = jnp.eye(size_head, dtype=jnp.float32) * jnp.exp(total_log) + jnp.einsum(
        "hcti,hctj->hcij", carried, beta_end, precision=highest
    )
    update = jnp.einsum("hcti,hctj->hcij", removal, beta_end, precision=highest) + jnp.einsum(
        "hcti,hctj->hcij", value_c, key_end, precision=highest
    )
    return (zero_out, reader, transfer, update)


def shards(
    stream,
    time_previous_token,
    channel_previous_token,
    head_state_initial,
    time_norm_gain,
    time_norm_bias,
    time_shift_weights,
    receptance,
    key_projection_matrix,
    value_projection_matrix,
    decay_first_factor,
    decay_second_factor,
    decay_channel_base,
    rate_first_factor,
    rate_second_factor,
    rate_channel_base,
    gate_first_factor,
    gate_second_factor,
    removal_key_scale,
    key_rate_scale,
    self_lookup_coefficient,
    head_group_gain,
    head_group_bias,
    time_output_weight,
    channel_norm_gain,
    channel_norm_bias,
    channel_shift_weight,
    channel_key_weight,
    channel_value_weight,
):
    sequence_place = stream.shape[0]
    device_portion = receptance.shape[1]
    head_number = device_portion // LANE_SPAN
    span_count = sequence_place // SPAN
    ctx_first = lax.axis_index("ctx") == 0
    normed = layer_norm(stream, time_norm_gain, time_norm_bias)
    arrived = passed_along(normed[-1:], "ctx", 1)
    previous = jnp.concatenate(
        [jnp.where(ctx_first, time_previous_token[None, :], arrived), normed[:-1]], axis=0
    )
    inputs = [mixed_input(normed, previous, time_shift_weights[position]) for position in range(6)]
    recept = jnp.dot(inputs[0], receptance, preferred_element_type=jnp.float32).astype(jnp.bfloat16)
    key_proj = jnp.dot(inputs[2], key_projection_matrix, preferred_element_type=jnp.float32).astype(
        jnp.bfloat16
    )
    value_proj = jnp.dot(
        inputs[3], value_projection_matrix, preferred_element_type=jnp.float32
    ).astype(jnp.bfloat16)
    decay_low = jnp.tanh(
        jnp.dot(inputs[1], decay_first_factor, preferred_element_type=jnp.float32)
    ).astype(jnp.bfloat16)
    decay_raw = decay_channel_base + jnp.dot(
        decay_low, decay_second_factor, preferred_element_type=jnp.float32
    )
    log_decay = -jnp.exp(-jax.nn.softplus(-decay_raw) - 0.5)
    rate_low = jnp.dot(inputs[4], rate_first_factor, preferred_element_type=jnp.float32).astype(
        jnp.bfloat16
    )
    rate = jax.nn.sigmoid(
        rate_channel_base
        + jnp.dot(rate_low, rate_second_factor, preferred_element_type=jnp.float32)
    )
    gate_low = jax.nn.sigmoid(
        jnp.dot(inputs[5], gate_first_factor, preferred_element_type=jnp.float32)
    ).astype(jnp.bfloat16)
    sigmoid_valve = jnp.dot(gate_low, gate_second_factor, preferred_element_type=jnp.float32)
    shape3 = (sequence_place, head_number, LANE_SPAN)
    key_rows = key_proj.astype(jnp.float32).reshape(shape3)
    scaled = key_rows * removal_key_scale.reshape(head_number, LANE_SPAN)
    norm_key = scaled * lax.rsqrt(jnp.sum(scaled * scaled, axis=-1, keepdims=True) + 1e-06)
    rate_rows = rate.reshape(shape3)
    lookup_corrected = key_rows * (
        1.0 + (rate_rows - 1.0) * key_rate_scale.reshape(head_number, LANE_SPAN)
    )
    acceptor_real = recept.astype(jnp.float32).reshape(shape3)
    payload_real = value_proj.astype(jnp.float32).reshape(shape3)

    def by_blocks(matrix):
        return matrix.reshape(span_count, SPAN, head_number, LANE_SPAN).transpose(2, 0, 1, 3)

    zero_out, reader, transfer, update = block_terms(
        by_blocks(acceptor_real),
        by_blocks(log_decay.reshape(shape3)),
        by_blocks(norm_key),
        by_blocks(rate_rows),
        by_blocks(lookup_corrected),
        by_blocks(payload_real),
    )
    identity = jnp.broadcast_to(
        jnp.eye(LANE_SPAN, dtype=jnp.float32), (head_number, LANE_SPAN, LANE_SPAN)
    )
    whole_transfer = identity
    whole_update = jnp.zeros((head_number, LANE_SPAN, LANE_SPAN), jnp.float32)
    for number in range(span_count):
        whole_update = compose(whole_update, transfer[:, number]) + update[:, number]
        whole_transfer = compose(whole_transfer, transfer[:, number])

    def relay(turn_number, incoming):
        leaving = compose(incoming, whole_transfer) + whole_update
        received = passed_along(leaving.astype(jnp.bfloat16), "ctx", 1).astype(leaving.dtype)
        return jnp.where(ctx_first, head_state_initial, received)

    entering = lax.fori_loop(0, lax.axis_size("ctx") - 1, relay, head_state_initial)
    current = entering
    pieces = []
    for number in range(span_count):
        pieces.append(
            zero_out[:, number]
            + jnp.einsum(
                "htj,hij->hti", reader[:, number], current, precision=lax.Precision.HIGHEST
            )
        )
        current = compose(current, transfer[:, number]) + update[:, number]
    wkv = jnp.stack(pieces, axis=1).transpose(1, 2, 0, 3).reshape(shape3)
    average = jnp.mean(wkv, axis=-1, keepdims=True)
    centered = wkv - average
    variance = jnp.mean(centered * centered, axis=-1, keepdims=True)
    lanewise_standardized = (centered * lax.rsqrt(variance + 0.00064)).reshape(
        sequence_place, device_portion
    ) * head_group_gain + head_group_bias
    diagonal_extra = (
        jnp.sum(
            acceptor_real
            * lookup_corrected
            * self_lookup_coefficient.reshape(head_number, LANE_SPAN),
            axis=-1,
            keepdims=True,
        )
        * payload_real
    )
    lagged_embedding = (
        (lanewise_standardized + diagonal_extra.reshape(sequence_place, device_portion))
        * sigmoid_valve
    ).astype(jnp.bfloat16)
    attended = lax.psum(
        jnp.dot(lagged_embedding, time_output_weight, preferred_element_type=jnp.float32).astype(
            jnp.bfloat16
        ),
        "tp",
    ).astype(jnp.float32)
    middle = (stream.astype(jnp.float32) + attended).astype(jnp.bfloat16)
    normed_next = layer_norm(middle, channel_norm_gain, channel_norm_bias)
    arrived_next = passed_along(normed_next[-1:], "ctx", 1)
    previous_next = jnp.concatenate(
        [jnp.where(ctx_first, channel_previous_token[None, :], arrived_next), normed_next[:-1]],
        axis=0,
    )
    channel_in = mixed_input(normed_next, previous_next, channel_shift_weight)
    expanded = jnp.maximum(
        jnp.dot(channel_in, channel_key_weight, preferred_element_type=jnp.float32), 0.0
    )
    hidden = (expanded * expanded).astype(jnp.bfloat16)
    channel = lax.psum(
        jnp.dot(hidden, channel_value_weight, preferred_element_type=jnp.float32).astype(
            jnp.bfloat16
        ),
        "tp",
    ).astype(jnp.float32)
    layer_out = (middle.astype(jnp.float32) + channel).astype(jnp.bfloat16)
    return layer_out


def solution(mesh):
    placed = (
        P("ctx", None),
        P(),
        P(),
        P("tp", None, None),
        P(),
        P(),
        P(),
        P(None, "tp"),
        P(None, "tp"),
        P(None, "tp"),
        P(),
        P(None, "tp"),
        P("tp"),
        P(),
        P(None, "tp"),
        P("tp"),
        P(),
        P(None, "tp"),
        P("tp"),
        P("tp"),
        P("tp"),
        P("tp"),
        P("tp"),
        P("tp", None),
        P(),
        P(),
        P(),
        P(None, "tp"),
        P("tp", None),
    )
    return jax.shard_map(
        shards, mesh=mesh, in_specs=placed, out_specs=P("ctx", None), check_vma=False
    )
```

profile of v0, /device:TPU:0, one launch (start us, length us, event | category | flops | bytes accessed | tf_op | source)
XLA Modules:
  0.0 740.4 jit_solution(5289552141893745384)
XLA Ops:
  15.8 5.2 collective-permute-start.1
  23.4 7.0 fusion.153
  36.0 7.3 broadcast_add_fusion
  48.0 8.6 %fusion.101 = f32[512,512]{0,1:T(8,128)S(1)} fusion(bf16[4096,512]{1,0:T(8,128)(2,1)} %param.39, bf16[512,4096]{1,0:T(8,128)(2,1)} %copy-done.29, f32[4096]{0:T(1024)} %bitcast.334, bf16[511,4096]{1,0:T(8,128)(2,1)} %bitcast.323, bf16[1,4096]{1,0:T(2,128)(2,1)} %copy-done.46), kind=kOutput, calls=%fused_computation.115 | convolution fusion | flops 2166882304 | bytes 13647872 | tf_op jit(solution)/shard_map/dot_general | solution.py:128
  58.4 8.7 %fusion.95 = f32[512,512]{0,1:T(8,128)} fusion(bf16[4096,512]{1,0:T(8,128)(2,1)} %param.38, bf16[512,4096]{1,0:T(8,128)(2,1)} %copy-done.29, f32[4096]{0:T(1024)} %bitcast.333, bf16[511,4096]{1,0:T(8,128)(2,1)} %bitcast.324, bf16[1,4096]{1,0:T(2,128)(2,1)} %copy-done.46), kind=kOutput, calls=%fused_computation.113 | convolution fusion | flops 2166882304 | bytes 13647872 | tf_op jit(solution)/shard_map/dot_general | solution.py:127
  75.7 7.2 bitcast_multiply_fusion.5
  83.2 5.4 fusion.201
  97.0 10.0 %fusion.177 = f32[8,8,64,64]{3,2,1,0:T(8,128)} fusion(f32[8,64,8,64]{3,1,0,2:T(8,128)} %copy.84, f32[8,8,64,64]{3,1,2,0:T(8,128)} %copy-done.1, f32[8,8,64]{2,1,0:T(8,128)S(1)} %get-tuple-element.61, f32[8,64,8,64]{3,1,0,2:T(8,128)} %copy.88, f32[8,64]{1,0:T(8,128)S(1)} %mul.310, f32[8,64,8,64]{3,1,0,2:T(8,128)} %copy.89), kind=kOutput, calls=%fused_computation.191 | convolution fusion | flops 203423744 | bytes 5261312 | tf_op jit(solution)/shard_map/hctj,hcsj->hcts/dot_general | solution.py:36
  107.0 5.2 fusion.178
  112.3 4.8 add_bitcast_fusion
  117.1 316.0 %custom-call.4 = f32[8,8,1,64,64]{3,4,2,1,0:T(8,128)} custom-call(f32[8,8,1,64,64]{4,3,2,1,0:T(8,128)} %add_bitcast_fusion), custom_call_target="InvertDiagBlocksLowerTriangular" | custom-call | tf_op jit(solution)/shard_map/jit(_solve_triangular)/vmap(vmap())/triangular_solve | solution.py:65
  442.1 4.1 multiply_add_fusion
  465.0 4.9 fusion.70
  469.9 21.0 %while.10 = (s32[]{:T(128)}, f32[8,64,64]{2,1,0:T(8,128)S(1)}, pred[]{:T(512)}, f32[8,64,64]{2,1,0:T(8,128)S(1)}, f32[8,64,64]{2,1,0:T(8,128)S(1)}, /*index=5*/f32[8,64,64]{2,1,0:T(8,128)S(1)}, s32[]{:T(128)}) while((s32[]{:T(128)}, f32[8,64,64]{2,1,0:T(8,128)S(1)}, pred[]{:T(512)}, f32[8,64,64]{2,1,0:T(8,128)S(1)}, ...), condition=%wide.region_5.6_spmd, body=%wide.region_4.5_spmd.sunk | while | flops 25296896 | bytes 1048694 | solution.py:188
  476.7 4.4 collective-permute-start
  484.0 4.4 collective-permute-start
  518.1 6.5 fusion.120
  524.6 8.0 %convolution_convert_fusion.1 = bf16[512,4096]{1,0:T(8,128)(2,1)} fusion(bf16[512,4096]{1,0:T(8,128)(2,1)} %param.54, bf16[512,256]{1,0:T(8,128)(2,1)} %fusion.120, bf16[256,512]{1,0:T(8,128)(2,1)S(1)} %copy-done.56, f32[512,512]{1,0:T(8,128)} %copy.116, bf16[512,512]{1,0:T(8,128)(2,1)} %fusion.104, f32[512,512]{1,0:T(8,128)} %copy.115, ...), kind=kOutput, calls=%fused_computation.42 | convolution fusion | flops 2286157824 | bytes 13635584 | tf_op jit(solution)/shard_map/dot_general | solution.py:221
  532.7 82.6 %all-reduce.3.cloned.1.call-done = bf16[512,4096]{1,0:T(8,128)(2,1)} async-done(((bf16[512,4096]{1,0:T(8,128)(2,1)}), bf16[512,4096]{1,0:T(8,128)(2,1)}) %all-reduce.3.cloned.1.call-update) | async-done | bytes 4194320 | tf_op jit(solution)/shard_map/psum | solution.py:220
  615.3 5.3 convert_reduce_fusion
  630.0 4.7 multiply_convert_fusion
  634.7 9.5 %convolution_convert_fusion = bf16[512,4096]{1,0:T(8,128)(2,1)} fusion(bf16[512,1024]{1,0:T(8,128)(2,1)S(1)} %multiply_convert_fusion, bf16[1024,4096]{1,0:T(8,128)(2,1)} %param.59), kind=kOutput, calls=%fused_computation.41 | convolution fusion | flops 4297064448 | bytes 13631488 | tf_op jit(solution)/shard_map/dot_general | solution.py:239
  644.3 81.9 %all-reduce.5.cloned.1.call-done = bf16[512,4096]{1,0:T(8,128)(2,1)} async-done(((bf16[512,4096]{1,0:T(8,128)(2,1)}), bf16[512,4096]{1,0:T(8,128)(2,1)}) %all-reduce.5.cloned.1.call-update) | async-done | bytes 4194320 | tf_op jit(solution)/shard_map/psum | solution.py:238
  726.1 7.2 fusion.17
  (231 shorter events, 116.8 us)
Async XLA Ops:
  6.5 511.5 %copy-start = (bf16[4096,256]{1,0:T(8,128)(2,1)S(1)}, bf16[4096,256]{1,0:T(8,128)(2,1)}, u32[]{:S(2)}) copy-start(bf16[4096,256]{1,0:T(8,128)(2,1)} %param.47) | copy-start | bytes 6291460
  6.5 608.8 %all-reduce.3.cloned.1.call-start = ((), (), s32[]{:S(2)}) async-start(), calls=%async_computation | async-start | bytes 8388608 | tf_op jit(solution)/shard_map/psum | solution.py:220
  11.4 9.7 %copy-start.35 = (bf16[6,4096]{1,0:T(8,128)(2,1)S(1)}, bf16[6,4096]{1,0:T(8,128)(2,1)}, u32[]{:S(2)}) copy-start(bf16[6,4096]{1,0:T(8,128)(2,1)} %param.37) | copy-start | bytes 147460
  11.4 11.1 %copy-start.52 = (f32[512]{0:T(512)S(1)}, f32[512]{0:T(512)}, u32[]{:S(2)}) copy-start(f32[512]{0:T(512)} %param.49) | copy-start | bytes 6148
  11.4 11.1 %copy-start.53 = (f32[512]{0:T(512)S(1)}, f32[512]{0:T(512)}, u32[]{:S(2)}) copy-start(f32[512]{0:T(512)} %param.50) | copy-start | bytes 6148
  11.4 11.2 %copy-start.54 = (f32[512]{0:T(512)S(1)}, f32[512]{0:T(512)}, u32[]{:S(2)}) copy-start(f32[512]{0:T(512)} %param.51) | copy-start | bytes 6148
  11.4 11.8 %copy-start.22 = (f32[8,64,64]{2,1,0:T(8,128)S(1)}, f32[8,64,64]{2,1,0:T(8,128)}, u32[]{:S(2)}) copy-start(f32[8,64,64]{2,1,0:T(8,128)} %param.34) | copy-start | bytes 393220
  11.5 11.9 %copy-start.50 = (bf16[4096]{0:T(1024)(128)(2,1)S(1)}, bf16[4096]{0:T(1024)(128)(2,1)}, u32[]{:S(2)}) copy-start(bf16[4096]{0:T(1024)(128)(2,1)} %param.32) | copy-start | bytes 24580
  15.8 7.5 %collective-permute-start.1 = (bf16[1,4096]{1,0:T(2,128)(2,1)S(1)}, bf16[1,4096]{1,0:T(2,128)(2,1)S(1)}, u32[]{:S(2)}, u32[]{:S(2)}) collective-permute-start(bf16[1,4096]{1,0:T(2,128)(2,1)S(1)} %slice.208), channel_id=1, source_target_pairs={{0,8},{8,16},{16,24},{1,9},{9,17},{17,25},{2,10},{10,18},{18,26},{... | collective-permute-start | bytes 24584 | tf_op jit(solution)/shard_map/ppermute | solution.py:13
  75.6 7.2 copy-start.2
  75.6 7.2 copy-start.7
  75.6 7.5 %copy-start.8 = (f32[8,64,8,64]{3,1,0,2:T(8,128)S(1)}, f32[8,64,8,64]{3,1,0,2:T(8,128)}, u32[]{:S(2)}) copy-start(f32[8,64,8,64]{3,1,0,2:T(8,128)} %copy.88) | copy-start | bytes 3145732
  97.0 10.0 %copy-start.3 = (f32[8,8,64,64]{3,1,2,0:T(8,128)S(1)}, f32[8,8,64,64]{3,1,2,0:T(8,128)}, u32[]{:S(2)}) copy-start(f32[8,8,64,64]{3,1,2,0:T(8,128)} %copy-done.1) | copy-start | bytes 3145732
  97.0 10.0 %copy-start.9 = (f32[8,64,8,64]{3,1,0,2:T(8,128)S(1)}, f32[8,64,8,64]{3,1,0,2:T(8,128)}, u32[]{:S(2)}) copy-start(f32[8,64,8,64]{3,1,0,2:T(8,128)} %copy.84) | copy-start | bytes 3145732
  97.0 10.0 %copy-start.17 = (f32[8,8,64,64]{3,2,1,0:T(8,128)S(1)}, f32[8,8,64,64]{3,2,1,0:T(8,128)}, u32[]{:S(2)}) copy-start(f32[8,8,64,64]{3,2,1,0:T(8,128)} %get-tuple-element.52) | copy-start | bytes 3145732
  446.2 11.6 %copy-start.11 = (f32[8,8,64,64]{3,2,1,0:T(8,128)}, f32[8,8,64,64]{3,2,1,0:T(8,128)S(1)}, u32[]{:S(2)}) copy-start(f32[8,8,64,64]{3,2,1,0:T(8,128)S(1)} %multiply_add_fusion) | copy-start | bytes 3145732
  470.3 6.0 collective-permute-start
  476.7 6.9 collective-permute-start
  484.0 6.9 collective-permute-start
  532.6 193.5 %all-reduce.5.cloned.1.call-start = ((), (), s32[]{:S(2)}) async-start(), calls=%async_computation.1 | async-start | bytes 8388608 | tf_op jit(solution)/shard_map/psum | solution.py:238
  615.3 14.7 %slice-start = ((s8[8388608]{0:T(1024)(128)(4,1)}), s8[4194304]{0:T(1024)(128)(4,1)S(1)}, s32[]{:S(2)}) async-start(s8[8388608]{0:T(1024)(128)(4,1)} %bitcast.337), calls=%async_computation.2 | async-start | bytes 8388608
  620.6 9.3 %slice-start.1 = ((s8[8388608]{0:T(1024)(128)(4,1)}), s8[4194304]{0:T(1024)(128)(4,1)S(1)}, s32[]{:S(2)}) async-start(s8[8388608]{0:T(1024)(128)(4,1)} %bitcast.337), calls=%async_computation.3 | async-start | bytes 8388608
  622.7 7.2 copy-start.51
  625.1 4.8 collective-permute-start.2
  (44 other events, 171.0 us)
Sparse Core Ops, SparseCore 0:
  532.8 82.4 all-reduce.2
  644.4 81.6 all-reduce.4
where the time goes:
time: 744 us; the launch traced here: 740 us
  other arithmetic  354 us (48%)
  waiting for transfers between devices  173 us (23%)
  matrix products  138 us (19%)
  local copies, waits for them, and re-layouts  38.9 us (5%)
  starting transfers between devices  21.1 us (3%)
  between operations  14.7 us (2%)
    another operation x2, other arithmetic, block_terms(): jax.scipy.linalg.solve_triangular(system, right_hand, lower=True, unit_di...  316 us
    psum x1, waiting for transfers between devices, shards(): lax.psum(jnp.dot(lagged_embedding, time_output_weight, preferred_element_...  82.6 us
    psum x1, waiting for transfers between devices, shards(): lax.psum(jnp.dot(hidden, channel_value_weight, preferred_element_type=jnp...  81.9 us
    dot_general x4, matrix products, pair_product(): jnp.einsum('hctj,hcsj->hcts', first, second, precision=lax.Precision.HIGH...  25.4 us
    ppermute x5, starting transfers between devices, passed_along(): return lax.ppermute(shard, axis, pairs)  21 us
    another operation x7, local copies, waits for them, and re-layouts, by_blocks(): matrix.reshape(span_count, SPAN, head_number, LANE_SPAN)  15.8 us
  transfers between devices with their start and end apart: 7, of which 6 were waited for; matrix products, arithmetic and copies ran while one was open for 0% of the time, Pallas kernels for 0%

commit v1 on v0

v1 whole, which is shorter than its diff:
```python
import functools

import jax
import jax.numpy as jnp
from jax import lax
from jax.experimental import pallas as pl
from jax.experimental.pallas import tpu as pltpu
from jax.sharding import PartitionSpec as P

LANE_SPAN = 64
SPAN = 64
PAIR = 2 * LANE_SPAN
F32 = jnp.float32
BF16 = jnp.bfloat16


def passed_along(shard, axis, by):
    length = lax.axis_size(axis)
    pairs = [(i, i + by) for i in range(length) if 0 <= i + by < length]
    return lax.ppermute(shard, axis, pairs)


def layer_norm(matrix, gain_vec, bias_vec):
    floats = matrix.astype(jnp.float32)
    average = jnp.mean(floats, axis=-1, keepdims=True)
    centered = floats - average
    variance = jnp.mean(centered * centered, axis=-1, keepdims=True)
    return (centered * lax.rsqrt(variance + 1e-05) * gain_vec + bias_vec).astype(jnp.bfloat16)


def mixed_input(normed, previous, weight_vec):
    current = normed.astype(jnp.float32)
    return (
        current + (previous.astype(jnp.float32) - current) * weight_vec.astype(jnp.float32)
    ).astype(jnp.bfloat16)


def mm(left, right):
    return jnp.dot(left.astype(BF16), right.astype(BF16), preferred_element_type=F32)


def mm_rt(left, right):
    return lax.dot_general(
        left.astype(BF16),
        right.astype(BF16),
        (((1,), (1,)), ((), ())),
        preferred_element_type=F32,
    )


def mm_lt(left, right):
    return lax.dot_general(
        left.astype(BF16),
        right.astype(BF16),
        (((0,), (0,)), ((), ())),
        preferred_element_type=F32,
    )


def split2(matrix):
    high = matrix.astype(BF16)
    return high, (matrix - high.astype(F32)).astype(BF16)


def head_ones():
    row = lax.broadcasted_iota(jnp.int32, (PAIR, PAIR), 0)
    col = lax.broadcasted_iota(jnp.int32, (PAIR, PAIR), 1)
    return ((row < LANE_SPAN) == (col < LANE_SPAN)).astype(BF16)


def head_sum(matrix, ones):
    high, low = split2(matrix)
    return jnp.dot(high, ones, preferred_element_type=F32) + jnp.dot(
        low, ones, preferred_element_type=F32
    )


def widened(matrix, same):
    return jnp.where(same, jnp.concatenate([matrix, matrix], axis=0), 0.0)


def folded(matrix):
    return matrix[:LANE_SPAN] + matrix[LANE_SPAN:]


def local_kernel(
    recept_ref, key_ref, value_ref, dlow_ref, rlow_ref, dsec_ref, rsec_ref, vec_ref,
    zero_ref, reader_ref, extra_ref, moved_ref,
    alpha_s, beta_s, logd_s, kadj_s,
):
    spans = recept_ref.shape[0] // SPAN
    ones = head_ones()
    vec = vec_ref[...]
    decay_raw = vec[0:1] + jnp.dot(dlow_ref[...], dsec_ref[...], preferred_element_type=F32)
    soft = jnp.maximum(-decay_raw, 0.0) + jnp.log1p(jnp.exp(-jnp.abs(decay_raw)))
    logd_s[...] = -jnp.exp(-soft - 0.5)
    rate = jax.nn.sigmoid(
        vec[1:2] + jnp.dot(rlow_ref[...], rsec_ref[...], preferred_element_type=F32)
    )
    keys = key_ref[...].astype(F32)
    scaled = keys * vec[2:3]
    norm_key = scaled * lax.rsqrt(head_sum(scaled * scaled, ones) + 1e-06)
    key_adj = keys * (1.0 + (rate - 1.0) * vec[3:4])
    recept_all = recept_ref[...].astype(F32)
    extra_ref[...] = (
        head_sum(recept_all * key_adj * vec[4:5], ones) * value_ref[...].astype(F32)
    )
    alpha_s[...] = -norm_key
    beta_s[...] = rate * norm_key
    kadj_s[...] = key_adj

    row = lax.broadcasted_iota(jnp.int32, (PAIR, PAIR), 0)
    col = lax.broadcasted_iota(jnp.int32, (PAIR, PAIR), 1)
    same = (row < LANE_SPAN) == (col < LANE_SPAN)
    strict = same & (row > col)
    inclusive = same & (row >= col)
    eye = (row == col).astype(F32)
    small_row = lax.broadcasted_iota(jnp.int32, (SPAN, SPAN), 0)
    small_col = lax.broadcasted_iota(jnp.int32, (SPAN, SPAN), 1)
    lower = (small_row >= small_col).astype(BF16)

    def levels():
        size = 1
        while size < SPAN:
            yield size, (row // (2 * size) == col // (2 * size)) & (row // size > col // size)
            size *= 2

    cuts = list(levels())

    chunks = []
    for number in range(spans):
        at = pl.ds(number * SPAN, SPAN)
        logd = logd_s[at, :]
        high, low = split2(logd)
        cumulative = jnp.dot(lower, high, preferred_element_type=F32) + jnp.dot(
            lower, low, preferred_element_type=F32
        )
        before = cumulative - logd
        total = cumulative[SPAN - 1 : SPAN, :]
        centre = 0.5 * total
        alpha = alpha_s[at, :]
        beta = beta_s[at, :]
        kadj = kadj_s[at, :]
        recept = recept_ref[at, :].astype(F32)
        grow = jnp.exp(centre - cumulative)
        half = jnp.exp(centre)
        decayed = jnp.exp(before - centre)
        reading = jnp.exp(cumulative - centre)
        left = alpha * decayed
        read = recept * reading
        b_side = beta * grow
        k_side = kadj * grow
        wide_b = widened(b_side, same).astype(BF16)
        wide_k = widened(k_side, same).astype(BF16)
        wide_l = widened(left, same).astype(BF16)
        wide_r = widened(read, same).astype(BF16)
        wide_v = widened(value_ref[at, :].astype(F32), same).astype(BF16)
        pairs = mm_rt(
            jnp.concatenate([wide_l, wide_r], axis=0), jnp.concatenate([wide_b, wide_k], axis=0)
        )
        system = jnp.where(strict, pairs[:PAIR, :PAIR], 0.0)
        key_pairs = jnp.where(strict, pairs[:PAIR, PAIR:], 0.0)
        read_rate = jnp.where(inclusive, pairs[PAIR:, :PAIR], 0.0).astype(BF16)
        read_key = jnp.where(inclusive, pairs[PAIR:, PAIR:], 0.0)
        values = mm(jnp.concatenate([key_pairs, read_key], axis=0), wide_v)
        inverse = eye + jnp.where(cuts[0][1], system, 0.0)
        for size, mask in cuts[1:]:
            inverse = inverse + mm(mm(inverse, jnp.where(mask, system, 0.0)), inverse)
        right_hand = jnp.concatenate([values[:PAIR], widened(left * half, same)], axis=1)
        solved = mm(inverse, right_hand).astype(BF16)
        seen = mm(read_rate, solved)
        zero = values[PAIR:] + seen[:, :PAIR]
        reader = (widened(read * half, same) + seen[:, PAIR:]).astype(BF16)
        wide_be = widened(b_side * half, same).astype(BF16)
        wide_ke = widened(k_side * half, same).astype(BF16)
        moved = mm_lt(solved, wide_be)
        update = moved[:PAIR] + mm_lt(wide_v, wide_ke)
        chunks.append((zero, reader, moved[PAIR:].astype(BF16), update, jnp.exp(total)))

    carry = jnp.concatenate([eye, jnp.zeros((PAIR, PAIR), F32)], axis=0)
    for number, (zero, reader, change, update, fade) in enumerate(chunks):
        at = pl.ds(number * SPAN, SPAN)
        carry16 = carry.astype(BF16)
        out = mm_rt(reader, carry16)
        reader_ref[at, :] = folded(out[:, :PAIR]).astype(BF16)
        zero_ref[at, :] = folded(zero + out[:, PAIR:])
        carry = carry * fade + jnp.dot(carry16, change, preferred_element_type=F32)
        carry = jnp.concatenate([carry[:PAIR], carry[PAIR:] + update], axis=0)
    moved_ref[0, 0] = folded(carry[:PAIR]).astype(BF16)
    moved_ref[0, 1] = folded(carry[PAIR:]).astype(BF16)


def wkv_local(recept, keys, values, dlow, rlow, dsec, rsec, vec):
    tokens, width = recept.shape
    count = width // PAIR
    by_pair = pl.BlockSpec((tokens, PAIR), lambda p: (0, p))
    whole = lambda a: pl.BlockSpec(a.shape, lambda p: (0, 0))
    cols = lambda a: pl.BlockSpec((a.shape[0], PAIR), lambda p: (0, p))
    return pl.pallas_call(
        local_kernel,
        grid=(count,),
        in_specs=[by_pair, by_pair, by_pair, whole(dlow), whole(rlow), cols(dsec), cols(rsec), cols(vec)],
        out_specs=[
            by_pair,
            by_pair,
            by_pair,
            pl.BlockSpec((1, 2, LANE_SPAN, PAIR), lambda p: (p, 0, 0, 0)),
        ],
        out_shape=[
            jax.ShapeDtypeStruct((tokens, width), F32),
            jax.ShapeDtypeStruct((tokens, width), BF16),
            jax.ShapeDtypeStruct((tokens, width), F32),
            jax.ShapeDtypeStruct((count, 2, LANE_SPAN, PAIR), BF16),
        ],
        scratch_shapes=[pltpu.VMEM((tokens, PAIR), F32)] * 4,
        compiler_params=pltpu.CompilerParams(vmem_limit_bytes=48 * 1024 * 1024),
        name="wkv_local",
    )(recept, keys, values, dlow, rlow, dsec, rsec, vec)


def finish_kernel(place_ref, zero_ref, reader_ref, extra_ref, glow_ref, gsec_ref, vec_ref, state_ref, *rest):
    moved_refs, out_ref = rest[:-1], rest[-1]
    ones = head_ones()
    row = lax.broadcasted_iota(jnp.int32, (PAIR, PAIR), 0)
    col = lax.broadcasted_iota(jnp.int32, (PAIR, PAIR), 1)
    same = (row < LANE_SPAN) == (col < LANE_SPAN)
    state = jnp.concatenate([state_ref[0], state_ref[1]], axis=1)
    place = place_ref[0]
    for back in range(len(moved_refs), 0, -1):
        moved = moved_refs[back - 1]
        wide = widened(moved[0, 0].astype(F32), same).astype(BF16)
        high, low = split2(state)
        after = (
            jnp.dot(high, wide, preferred_element_type=F32)
            + jnp.dot(low, wide, preferred_element_type=F32)
            + moved[0, 1].astype(F32)
        )
        state = jnp.where(place >= back, after, state)
    wkv = zero_ref[...] + mm_rt(reader_ref[...], widened(state, same))
    scale = 1.0 / LANE_SPAN
    centered = wkv - head_sum(wkv, ones) * scale
    variance = head_sum(centered * centered, ones) * scale
    vec = vec_ref[...]
    normal = centered * lax.rsqrt(variance + 0.00064) * vec[5:6] + vec[6:7]
    gate = jnp.dot(glow_ref[...], gsec_ref[...], preferred_element_type=F32)
    out_ref[...] = ((normal + extra_ref[...]) * gate).astype(BF16)


def wkv_finish(place, zero, reader, extra, glow, gsec, vec, state, moved):
    tokens, width = zero.shape
    count = width // PAIR
    by_pair = pl.BlockSpec((tokens, PAIR), lambda p: (0, p))
    whole = lambda a: pl.BlockSpec(a.shape, lambda p: (0, 0))
    cols = lambda a: pl.BlockSpec((a.shape[0], PAIR), lambda p: (0, p))
    return pl.pallas_call(
        finish_kernel,
        grid=(count,),
        in_specs=[
            pl.BlockSpec(memory_space=pltpu.SMEM),
            by_pair,
            by_pair,
            by_pair,
            whole(glow),
            cols(gsec),
            cols(vec),
            pl.BlockSpec((2, LANE_SPAN, LANE_SPAN), lambda p: (p, 0, 0)),
        ]
        + [pl.BlockSpec((1, 2, LANE_SPAN, PAIR), lambda p: (p, 0, 0, 0))] * len(moved),
        out_specs=by_pair,
        out_shape=jax.ShapeDtypeStruct((tokens, width), BF16),
        compiler_params=pltpu.CompilerParams(vmem_limit_bytes=48 * 1024 * 1024),
        name="wkv_finish",
    )(place, zero, reader, extra, glow, gsec, vec, state, *moved)


def shards(
    stream,
    time_previous_token,
    channel_previous_token,
    head_state_initial,
    time_norm_gain,
    time_norm_bias,
    time_shift_weights,
    receptance,
    key_projection_matrix,
    value_projection_matrix,
    decay_first_factor,
    decay_second_factor,
    decay_channel_base,
    rate_first_factor,
    rate_second_factor,
    rate_channel_base,
    gate_first_factor,
    gate_second_factor,
    removal_key_scale,
    key_rate_scale,
    self_lookup_coefficient,
    head_group_gain,
    head_group_bias,
    time_output_weight,
    channel_norm_gain,
    channel_norm_bias,
    channel_shift_weight,
    channel_key_weight,
    channel_value_weight,
):
    normed = layer_norm(stream, time_norm_gain, time_norm_bias)
    ctx_place = lax.axis_index("ctx")
    ctx_first = ctx_place == 0
    arrived = passed_along(normed[-1:], "ctx", 1)
    previous = jnp.concatenate(
        [jnp.where(ctx_first, time_previous_token[None, :], arrived), normed[:-1]], axis=0
    )
    inputs = [mixed_input(normed, previous, time_shift_weights[position]) for position in range(6)]
    recept = jnp.dot(inputs[0], receptance, preferred_element_type=F32).astype(BF16)
    keys = jnp.dot(inputs[2], key_projection_matrix, preferred_element_type=F32).astype(BF16)
    values = jnp.dot(inputs[3], value_projection_matrix, preferred_element_type=F32).astype(BF16)
    decay_low = jnp.tanh(
        jnp.dot(inputs[1], decay_first_factor, preferred_element_type=F32)
    ).astype(BF16)
    rate_low = jnp.dot(inputs[4], rate_first_factor, preferred_element_type=F32).astype(BF16)
    gate_low = jax.nn.sigmoid(
        jnp.dot(inputs[5], gate_first_factor, preferred_element_type=F32)
    ).astype(BF16)
    vec = jnp.stack(
        [
            decay_channel_base,
            rate_channel_base,
            removal_key_scale,
            key_rate_scale,
            self_lookup_coefficient,
            head_group_gain,
            head_group_bias,
            head_group_bias,
        ]
    )
    zero, reader, extra, moved = wkv_local(
        recept, keys, values, decay_low, rate_low, decay_second_factor, rate_second_factor, vec
    )
    arrivals = [passed_along(moved, "ctx", by) for by in range(1, lax.axis_size("ctx"))]
    lagged_embedding = wkv_finish(
        ctx_place.reshape(1).astype(jnp.int32),
        zero,
        reader,
        extra,
        gate_low,
        gate_second_factor,
        vec,
        head_state_initial,
        arrivals,
    )
    attended = lax.psum(
        jnp.dot(lagged_embedding, time_output_weight, preferred_element_type=jnp.float32).astype(
            jnp.bfloat16
        ),
        "tp",
    ).astype(jnp.float32)
    middle = (stream.astype(jnp.float32) + attended).astype(jnp.bfloat16)
    normed_next = layer_norm(middle, channel_norm_gain, channel_norm_bias)
    arrived_next = passed_along(normed_next[-1:], "ctx", 1)
    previous_next = jnp.concatenate(
        [jnp.where(ctx_first, channel_previous_token[None, :], arrived_next), normed_next[:-1]],
        axis=0,
    )
    channel_in = mixed_input(normed_next, previous_next, channel_shift_weight)
    expanded = jnp.maximum(
        jnp.dot(channel_in, channel_key_weight, preferred_element_type=jnp.float32), 0.0
    )
    hidden = (expanded * expanded).astype(jnp.bfloat16)
    channel = lax.psum(
        jnp.dot(hidden, channel_value_weight, preferred_element_type=jnp.float32).astype(
            jnp.bfloat16
        ),
        "tp",
    ).astype(jnp.float32)
    layer_out = (middle.astype(jnp.float32) + channel).astype(jnp.bfloat16)
    return layer_out


def solution(mesh):
    placed = (
        P("ctx", None),
        P(),
        P(),
        P("tp", None, None),
        P(),
        P(),
        P(),
        P(None, "tp"),
        P(None, "tp"),
        P(None, "tp"),
        P(),
        P(None, "tp"),
        P("tp"),
        P(),
        P(None, "tp"),
        P("tp"),
        P(),
        P(None, "tp"),
        P("tp"),
        P("tp"),
        P("tp"),
        P("tp"),
        P("tp"),
        P("tp", None),
        P(),
        P(),
        P(),
        P(None, "tp"),
        P("tp", None),
    )
    return jax.shard_map(
        shards, mesh=mesh, in_specs=placed, out_specs=P("ctx", None), check_vma=False
    )
```

time: 744 us -> 335 us (0.45)
  other arithmetic: 354 us -> 25 us
  matrix products: 138 us -> 37.5 us
  Pallas kernels: 0 us -> 68.2 us
  local copies, waits for them, and re-layouts: 38.9 us -> 2.26 us
    another operation x3 -> x0, other arithmetic: 318 us -> none  [the longest x2 316 us: block_terms(): jax.scipy.linalg.solve_triangular(system, right_hand, lower=True, unit_di...]
    dot_general x51 -> x6, matrix products: 112 us -> 18.9 us  [the longest x1 5.8 us: shards(): jnp.dot(inputs[4], rate_first_factor, preferred_element_type=F32)]
    pallas_call x0 -> x2, Pallas kernels: none -> 68.2 us  [the longest x1 63.3 us: wkv_local(): pl.pallas_call(local_kernel, grid=(count,), in_specs=[by_pair, by_pair, b...]
    another operation x7 -> x1, local copies, waits for them, and re-layouts: 15.8 us -> 0.04 us  [shards(): jnp.stack([decay_channel_base, rate_channel_base, removal_key_scale, key_...]
    mul x3 -> x0, other arithmetic: 8.61 us -> none  [the longest x1 7.19 us: block_terms(): beta_side = beta * jnp.exp(centre - cumulative)]
    reshape x3 -> x0, local copies, waits for them, and re-layouts: 7.75 us -> none  [the longest x2 4.67 us: shards(): key_rows = key_proj.astype(jnp.float32).reshape(shape3)]
  transfers between devices with their start and end apart: 7 -> 7, of which waited for: 6 -> 5; matrix products, arithmetic and copies ran while one was open for 0% -> 1% of each run, Pallas kernels for 0% -> 0%
where the time goes in v1:
time: 335 us
  waiting for transfers between devices  169 us (50%)
  Pallas kernels  68.2 us (20%)
  matrix products  37.5 us (11%)
  other arithmetic  25 us (7%)
  starting transfers between devices  18.9 us (6%)
  between operations  14 us (4%)
    psum x1, waiting for transfers between devices, shards(): lax.psum(jnp.dot(lagged_embedding, time_output_weight, preferred_element_...  84.5 us
    psum x1, waiting for transfers between devices, shards(): lax.psum(jnp.dot(hidden, channel_value_weight, preferred_element_type=jnp...  81.9 us
    pallas_call x1, Pallas kernels, wkv_local(): pl.pallas_call(local_kernel, grid=(count,), in_specs=[by_pair, by_pair, b...  63.3 us
    ppermute x5, starting transfers between devices, passed_along(): return lax.ppermute(shard, axis, pairs)  18.5 us
    dot_general x1, matrix products, shards(): jnp.dot(hidden, channel_value_weight, preferred_element_type=jnp.float32)  9.48 us
    reduce_sum x2, other arithmetic, layer_norm(): average = jnp.mean(floats, axis=-1, keepdims=True)  8.29 us
    convert_element_type x1, other arithmetic, shards(): layer_out = (middle.astype(jnp.float32) + channel).astype(jnp.bfloat16)  7.25 us
  transfers between devices with their start and end apart: 7, of which 5 were waited for; matrix products, arithmetic and copies ran while one was open for 1% of the time, Pallas kernels for 0%

profile of v1, /device:TPU:0, one launch (start us, length us, event | category | flops | bytes accessed | tf_op | source)
XLA Modules:
  0.0 335.2 jit_solution(5816272766174640489)
XLA Ops:
  6.7 3.0 convert_reduce_fusion.1
  9.7 3.5 %fusion.8 = f32[512]{0:T(512)S(1)} fusion(bf16[512,4096]{1,0:T(8,128)(2,1)} %param.29, f32[512]{0:T(512)S(1)} %broadcast_multiply_fusion.1), kind=kLoop, calls=%fused_computation.23 | loop fusion | flops 8388096 | bytes 4198400 | tf_op jit(solution)/shard_map/reduce_sum | solution.py:27
  13.3 2.3 fusion.11
  15.5 2.0 copy-done.8
  17.6 5.1 %collective-permute-start = (bf16[1,4096]{1,0:T(2,128)(2,1)S(1)}, bf16[1,4096]{1,0:T(2,128)(2,1)S(1)}, u32[]{:S(2)}, u32[]{:S(2)}) collective-permute-start(bf16[1,4096]{1,0:T(2,128)(2,1)S(1)} %slice.40), channel_id=1, source_target_pairs={{0,8},{8,16},{16,24},{1,9},{9,17},{17,25},{2,10},{10,18},{18,26},{... | collective-permute-start | bytes 24584 | tf_op jit(solution)/shard_map/ppermute | solution.py:20
  24.0 5.8 %fusion.76.rlow_ref = bf16[512,128]{1,0:T(8,128)(2,1)S(1)} fusion(bf16[4096,128]{1,0:T(8,128)(2,1)S(1)} %copy-done.29, bf16[512,4096]{1,0:T(8,128)(2,1)} %copy-done.8, f32[4096]{0:T(1024)S(1)} %bitcast.39, bf16[511,4096]{1,0:T(8,128)(2,1)} %bitcast.27, bf16[1,4096]{1,0:T(2,128)(2,1)S(1)} %broadcast_select_fusion.1), kind=kOutput, calls=%fused_computation.66 | convolution fusion | flops 555810816 | bytes 9584640 | tf_op jit(solution)/shard_map/dot_general | solution.py:321
  29.9 3.0 fusion.73.dlow_ref
  32.9 2.3 fusion.52.value_ref
  35.3 2.5 fusion.49.key_ref
  37.8 2.5 fusion.46.recept_ref
  40.3 63.3 %wkv_local.1 = (f32[512,512]{1,0:T(8,128)S(1)}, bf16[512,512]{1,0:T(8,128)(2,1)S(1)}, f32[512,512]{1,0:T(8,128)S(1)}, bf16[4,2,64,128]{3,2,1,0:T(8,128)(2,1)S(1)}) custom-call(bf16[512,512]{1,0:T(8,128)(2,1)S(1)} %fusion.46.recept_ref, bf16[512,512]{1,0:T(8,128)(2,1)S(1)} %fusion.49.key_ref, bf16[512,512]{1,0:T(8,128)(2,1)S(1)} %fusion.52.value_ref, ...), custom_call_target="tpu_custom_call" | custom-call | tf_op jit(solution)/shard_map/wkv_local/pallas_call | solution.py:199
  103.6 6.2 %collective-permute-start.3 = (bf16[4,2,64,128]{3,2,1,0:T(8,128)(2,1)S(1)}, bf16[4,2,64,128]{3,2,1,0:T(8,128)(2,1)S(1)}, u32[]{:S(2)}, u32[]{:S(2)}) collective-permute-start(bf16[4,2,64,128]{3,2,1,0:T(8,128)(2,1)S(1)} %get-tuple-element.12), channel_id=1, source_target_pairs={{0,24},{1,25},{2,26},{3,27},{4,28},{5,29},{6,30},{7,31}} | collective-permute-start | bytes 393224 | tf_op jit(solution)/shard_map/ppermute | solution.py:20
  111.1 2.5 collective-permute-start.1
  113.7 2.8 fusion.67.glow_ref
  117.1 4.9 %wkv_finish.1 = bf16[512,512]{1,0:T(8,128)(2,1)S(1)} custom-call(s32[1]{0:T(128)} %bitcast.place_ref, f32[512,512]{1,0:T(8,128)S(1)} %get-tuple-element.9.zero_ref, bf16[512,512]{1,0:T(8,128)(2,1)S(1)} %get-tuple-element.10.reader_ref, f32[512,512]{1,0:T(8,128)S(1)} %get-tuple-element.11.extra_ref, bf16[512,256]{1,0:T(8,128)(2,1)S(1)} %fusion.67.glow_ref, ...), custom_call_target="tpu_custom_call" | custom-call | tf_op jit(solution)/shard_map/wkv_finish/pallas_call | solution.py:255
  122.0 4.4 %convolution_convert_fusion.1 = bf16[512,4096]{1,0:T(8,128)(2,1)} fusion(bf16[512,512]{1,0:T(8,128)(2,1)S(1)} %wkv_finish.1, bf16[512,4096]{1,0:T(8,128)(2,1)S(1)} %copy-done.28), kind=kOutput, calls=%fused_computation.38 | convolution fusion | flops 2149580800 | bytes 8912896 | tf_op jit(solution)/shard_map/dot_general | solution.py:353
  126.7 84.5 %all-reduce.3.cloned.1.call-done = bf16[512,4096]{1,0:T(8,128)(2,1)} async-done(((bf16[512,4096]{1,0:T(8,128)(2,1)}), bf16[512,4096]{1,0:T(8,128)(2,1)}) %all-reduce.3.cloned.1.call-update) | async-done | bytes 4194320 | tf_op jit(solution)/shard_map/psum | solution.py:352
  211.1 5.3 %convert_reduce_fusion = (f32[512]{0:T(512)S(1)}, bf16[512,4096]{1,0:T(8,128)(2,1)S(1)}) fusion(bf16[512,4096]{1,0:T(8,128)(2,1)} %all-reduce.3.cloned.1.call-done, bf16[512,4096]{1,0:T(8,128)(2,1)} %param.29), kind=kLoop, calls=%fused_computation.9 | loop fusion | flops 12582400 | bytes 12584960 | tf_op jit(solution)/shard_map/reduce_sum | solution.py:25
  217.8 2.3 fusion.7
  220.1 3.4 %collective-permute-start.4 = (bf16[1,4096]{1,0:T(2,128)(2,1)S(1)}, bf16[1,4096]{1,0:T(2,128)(2,1)S(1)}, u32[]{:S(2)}, u32[]{:S(2)}) collective-permute-start(bf16[1,4096]{1,0:T(2,128)(2,1)S(1)} %slice.42), channel_id=1, source_target_pairs={{0,8},{8,16},{16,24},{1,9},{9,17},{17,25},{2,10},{10,18},{18,26},{... | collective-permute-start | bytes 24584 | tf_op jit(solution)/shard_map/ppermute | solution.py:20
  225.0 4.7 %multiply_convert_fusion = bf16[512,1024]{1,0:T(8,128)(2,1)S(1)} fusion(bf16[4096,1024]{1,0:T(8,128)(2,1)S(1)} %bitcast.49, bf16[512,4096]{1,0:T(8,128)(2,1)S(1)} %fusion.7, bf16[511,4096]{1,0:T(8,128)(2,1)S(1)} %bitcast.33, bf16[1,4096]{1,0:T(2,128)(2,1)S(1)} %broadcast_select_fusion, f32[4096]{0:T(1024)S(1)} %convert_element_type.134), kind=kOutput, calls=%fused_computation.55 | convolution fusion | flops 4315414528 | bytes 17842176 | tf_op jit(solution)/shard_map/dot_general | solution.py:367
  229.8 9.5 %convolution_convert_fusion = bf16[512,4096]{1,0:T(8,128)(2,1)} fusion(bf16[512,1024]{1,0:T(8,128)(2,1)S(1)} %multiply_convert_fusion, bf16[1024,4096]{1,0:T(8,128)(2,1)} %param.57), kind=kOutput, calls=%fused_computation.37 | convolution fusion | flops 4297064448 | bytes 13631488 | tf_op jit(solution)/shard_map/dot_general | solution.py:371
  239.3 81.9 %all-reduce.5.cloned.1.call-done = bf16[512,4096]{1,0:T(8,128)(2,1)} async-done(((bf16[512,4096]{1,0:T(8,128)(2,1)}), bf16[512,4096]{1,0:T(8,128)(2,1)}) %all-reduce.5.cloned.1.call-update) | async-done | bytes 4194320 | tf_op jit(solution)/shard_map/psum | solution.py:370
  321.1 7.2 %fusion.15 = bf16[512,4096]{1,0:T(8,128)(2,1)} fusion(bf16[512,4096]{1,0:T(8,128)(2,1)} %copy-done.6, bf16[512,4096]{1,0:T(8,128)(2,1)} %all-reduce.5.cloned.1.call-done), kind=kLoop, calls=%fused_computation.30 | loop fusion | flops 8388608 | bytes 12582912 | tf_op jit(solution)/shard_map/convert_element_type | solution.py:376
  (88 shorter events, 6.3 us)
Async XLA Ops:
  6.5 107.1 %copy-start = (bf16[4096,256]{1,0:T(8,128)(2,1)S(1)}, bf16[4096,256]{1,0:T(8,128)(2,1)}, u32[]{:S(2)}) copy-start(bf16[4096,256]{1,0:T(8,128)(2,1)} %param.45) | copy-start | bytes 6291460
  6.5 16.2 %copy-start.10 = (bf16[6,4096]{1,0:T(8,128)(2,1)S(1)}, bf16[6,4096]{1,0:T(8,128)(2,1)}, u32[]{:S(2)}) copy-start(bf16[6,4096]{1,0:T(8,128)(2,1)} %param.35) | copy-start | bytes 147460
  6.5 16.3 %copy-start.16 = (f32[512]{0:T(512)S(1)}, f32[512]{0:T(512)}, u32[]{:S(2)}) copy-start(f32[512]{0:T(512)} %param.51) | copy-start | bytes 6148
  6.5 16.3 %copy-start.24 = (f32[512]{0:T(512)S(1)}, f32[512]{0:T(512)}, u32[]{:S(2)}) copy-start(f32[512]{0:T(512)} %param.50) | copy-start | bytes 6148
  6.6 16.3 %copy-start.23 = (f32[512]{0:T(512)S(1)}, f32[512]{0:T(512)}, u32[]{:S(2)}) copy-start(f32[512]{0:T(512)} %param.49) | copy-start | bytes 6148
  6.6 16.3 %copy-start.22 = (f32[512]{0:T(512)S(1)}, f32[512]{0:T(512)}, u32[]{:S(2)}) copy-start(f32[512]{0:T(512)} %param.48) | copy-start | bytes 6148
  6.6 16.3 %copy-start.21 = (f32[512]{0:T(512)S(1)}, f32[512]{0:T(512)}, u32[]{:S(2)}) copy-start(f32[512]{0:T(512)} %param.47) | copy-start | bytes 6148
  6.6 16.3 %copy-start.20 = (f32[512]{0:T(512)S(1)}, f32[512]{0:T(512)}, u32[]{:S(2)}) copy-start(f32[512]{0:T(512)} %param.44) | copy-start | bytes 6148
  6.6 16.3 %copy-start.19 = (f32[512]{0:T(512)S(1)}, f32[512]{0:T(512)}, u32[]{:S(2)}) copy-start(f32[512]{0:T(512)} %param.41) | copy-start | bytes 6148
  6.6 17.3 %copy-start.17 = (bf16[4096]{0:T(1024)(128)(2,1)S(1)}, bf16[4096]{0:T(1024)(128)(2,1)}, u32[]{:S(2)}) copy-start(bf16[4096]{0:T(1024)(128)(2,1)} %param.30) | copy-start | bytes 24580
  6.6 17.4 %copy-start.29 = (bf16[4096,128]{1,0:T(8,128)(2,1)S(1)}, bf16[4096,128]{1,0:T(8,128)(2,1)}, u32[]{:S(2)}) copy-start(bf16[4096,128]{1,0:T(8,128)(2,1)} %param.42) | copy-start | bytes 3145732
  6.6 204.5 %all-reduce.3.cloned.1.call-start = ((), (), s32[]{:S(2)}) async-start(), calls=%async_computation | async-start | bytes 8388608 | tf_op jit(solution)/shard_map/psum | solution.py:352
  17.6 6.4 %collective-permute-start = (bf16[1,4096]{1,0:T(2,128)(2,1)S(1)}, bf16[1,4096]{1,0:T(2,128)(2,1)S(1)}, u32[]{:S(2)}, u32[]{:S(2)}) collective-permute-start(bf16[1,4096]{1,0:T(2,128)(2,1)S(1)} %slice.40), channel_id=1, source_target_pairs={{0,8},{8,16},{16,24},{1,9},{9,17},{17,25},{2,10},{10,18},{18,26},{... | collective-permute-start | bytes 24584 | tf_op jit(solution)/shard_map/ppermute | solution.py:20
  103.6 12.9 %collective-permute-start.3 = (bf16[4,2,64,128]{3,2,1,0:T(8,128)(2,1)S(1)}, bf16[4,2,64,128]{3,2,1,0:T(8,128)(2,1)S(1)}, u32[]{:S(2)}, u32[]{:S(2)}) collective-permute-start(bf16[4,2,64,128]{3,2,1,0:T(8,128)(2,1)S(1)} %get-tuple-element.12), channel_id=1, source_target_pairs={{0,24},{1,25},{2,26},{3,27},{4,28},{5,29},{6,30},{7,31}} | collective-permute-start | bytes 393224 | tf_op jit(solution)/shard_map/ppermute | solution.py:20
  109.8 6.7 %collective-permute-start.2 = (bf16[4,2,64,128]{3,2,1,0:T(8,128)(2,1)S(1)}, bf16[4,2,64,128]{3,2,1,0:T(8,128)(2,1)S(1)}, u32[]{:S(2)}, u32[]{:S(2)}) collective-permute-start(bf16[4,2,64,128]{3,2,1,0:T(8,128)(2,1)S(1)} %get-tuple-element.12), channel_id=1, source_target_pairs={{0,16},{8,24},{1,17},{9,25},{2,18},{10,26},{3,19},{11,27},{4,20},{... | collective-permute-start | bytes 393224 | tf_op jit(solution)/shard_map/ppermute | solution.py:20
  111.1 5.9 %collective-permute-start.1 = (bf16[4,2,64,128]{3,2,1,0:T(8,128)(2,1)S(1)}, bf16[4,2,64,128]{3,2,1,0:T(8,128)(2,1)S(1)}, u32[]{:S(2)}, u32[]{:S(2)}) collective-permute-start(bf16[4,2,64,128]{3,2,1,0:T(8,128)(2,1)S(1)} %get-tuple-element.12), channel_id=1, source_target_pairs={{0,8},{8,16},{16,24},{1,9},{9,17},{17,25},{2,10},{10,18},{18,26},{... | collective-permute-start | bytes 393224 | tf_op jit(solution)/shard_map/ppermute | solution.py:20
  126.3 91.4 %copy-start.13 = (f32[4096]{0:T(1024)S(1)}, f32[4096]{0:T(1024)}, u32[]{:S(2)}) copy-start(f32[4096]{0:T(1024)} %param.54) | copy-start | bytes 49156
  126.4 91.4 %copy-start.14 = (f32[4096]{0:T(1024)S(1)}, f32[4096]{0:T(1024)}, u32[]{:S(2)}) copy-start(f32[4096]{0:T(1024)} %param.53) | copy-start | bytes 49156
  126.4 194.7 %all-reduce.5.cloned.1.call-start = ((), (), s32[]{:S(2)}) async-start(), calls=%async_computation.1 | async-start | bytes 8388608 | tf_op jit(solution)/shard_map/psum | solution.py:370
  211.1 13.8 %slice-start = ((s8[8388608]{0:T(1024)(128)(4,1)}), s8[4194304]{0:T(1024)(128)(4,1)S(1)}, s32[]{:S(2)}) async-start(s8[8388608]{0:T(1024)(128)(4,1)} %bitcast.48), calls=%async_computation.2 | async-start | bytes 8388608
  216.5 13.3 %copy-start.6 = (bf16[512,4096]{1,0:T(8,128)(2,1)}, bf16[512,4096]{1,0:T(8,128)(2,1)S(1)}, u32[]{:S(2)}) copy-start(bf16[512,4096]{1,0:T(8,128)(2,1)S(1)} %get-tuple-element.14) | copy-start | bytes 12582916
  216.5 8.5 %slice-start.1 = ((s8[8388608]{0:T(1024)(128)(4,1)}), s8[4194304]{0:T(1024)(128)(4,1)S(1)}, s32[]{:S(2)}) async-start(s8[8388608]{0:T(1024)(128)(4,1)} %bitcast.48), calls=%async_computation.3 | async-start | bytes 8388608
  220.1 4.8 %collective-permute-start.4 = (bf16[1,4096]{1,0:T(2,128)(2,1)S(1)}, bf16[1,4096]{1,0:T(2,128)(2,1)S(1)}, u32[]{:S(2)}, u32[]{:S(2)}) collective-permute-start(bf16[1,4096]{1,0:T(2,128)(2,1)S(1)} %slice.42), channel_id=1, source_target_pairs={{0,8},{8,16},{16,24},{1,9},{9,17},{17,25},{2,10},{10,18},{18,26},{... | collective-permute-start | bytes 24584 | tf_op jit(solution)/shard_map/ppermute | solution.py:20
  239.2 89.1 %copy-start.1 = (bf16[4096,256]{1,0:T(8,128)(2,1)S(1)}, bf16[4096,256]{1,0:T(8,128)(2,1)}, u32[]{:S(2)}) copy-start(bf16[4096,256]{1,0:T(8,128)(2,1)} %param.45) | copy-start | bytes 6291460
  (16 other events, 77.2 us)
Sparse Core Ops, SparseCore 0:
  126.5 84.6 all-reduce.2
  239.4 81.6 all-reduce.4

commit v2 on v1

--- a/solution.py
+++ b/solution.py
@@ -127,7 +127,7 @@
 
     cuts = list(levels())
 
-    chunks = []
+    stage = []
     for number in range(spans):
         at = pl.ds(number * SPAN, SPAN)
         logd = logd_s[at, :]
@@ -138,44 +138,61 @@
         before = cumulative - logd
         total = cumulative[SPAN - 1 : SPAN, :]
         centre = 0.5 * total
-        alpha = alpha_s[at, :]
-        beta = beta_s[at, :]
-        kadj = kadj_s[at, :]
-        recept = recept_ref[at, :].astype(F32)
         grow = jnp.exp(centre - cumulative)
         half = jnp.exp(centre)
-        decayed = jnp.exp(before - centre)
-        reading = jnp.exp(cumulative - centre)
-        left = alpha * decayed
-        read = recept * reading
-        b_side = beta * grow
-        k_side = kadj * grow
+        left = alpha_s[at, :] * jnp.exp(before - centre)
+        read = recept_ref[at, :].astype(F32) * jnp.exp(cumulative - centre)
+        b_side = beta_s[at, :] * grow
+        k_side = kadj_s[at, :] * grow
         wide_b = widened(b_side, same).astype(BF16)
         wide_k = widened(k_side, same).astype(BF16)
         wide_l = widened(left, same).astype(BF16)
         wide_r = widened(read, same).astype(BF16)
-        wide_v = widened(value_ref[at, :].astype(F32), same).astype(BF16)
         pairs = mm_rt(
             jnp.concatenate([wide_l, wide_r], axis=0), jnp.concatenate([wide_b, wide_k], axis=0)
         )
         system = jnp.where(strict, pairs[:PAIR, :PAIR], 0.0)
-        key_pairs = jnp.where(strict, pairs[:PAIR, PAIR:], 0.0)
+        both = jnp.concatenate(
+            [
+                jnp.where(strict, pairs[:PAIR, PAIR:], 0.0),
+                jnp.where(inclusive, pairs[PAIR:, PAIR:], 0.0),
+            ],
+            axis=0,
+        ).astype(BF16)
         read_rate = jnp.where(inclusive, pairs[PAIR:, :PAIR], 0.0).astype(BF16)
-        read_key = jnp.where(inclusive, pairs[PAIR:, PAIR:], 0.0)
-        values = mm(jnp.concatenate([key_pairs, read_key], axis=0), wide_v)
-        inverse = eye + jnp.where(cuts[0][1], system, 0.0)
-        for size, mask in cuts[1:]:
-            inverse = inverse + mm(mm(inverse, jnp.where(mask, system, 0.0)), inverse)
-        right_hand = jnp.concatenate([values[:PAIR], widened(left * half, same)], axis=1)
-        solved = mm(inverse, right_hand).astype(BF16)
-        seen = mm(read_rate, solved)
-        zero = values[PAIR:] + seen[:, :PAIR]
-        reader = (widened(read * half, same) + seen[:, PAIR:]).astype(BF16)
-        wide_be = widened(b_side * half, same).astype(BF16)
-        wide_ke = widened(k_side * half, same).astype(BF16)
-        moved = mm_lt(solved, wide_be)
-        update = moved[:PAIR] + mm_lt(wide_v, wide_ke)
-        chunks.append((zero, reader, moved[PAIR:].astype(BF16), update, jnp.exp(total)))
+        stage.append(
+            dict(
+                at=at, half=half, total=total, system=system.astype(BF16), both=both,
+                read_rate=read_rate, left=left, read=read, b_side=b_side, k_side=k_side,
+                inverse=eye + jnp.where(cuts[0][1], system, 0.0),
+            )
+        )
+    for item in stage:
+        item["wide_v"] = widened(value_ref[item["at"], :].astype(F32), same).astype(BF16)
+        item["values"] = mm(item["both"], item["wide_v"])
+    zero16 = jnp.zeros((PAIR, PAIR), BF16)
+    for size, mask in cuts[1:]:
+        for item in stage:
+            item["inv16"] = item["inverse"].astype(BF16)
+            item["step"] = mm(item["inv16"], jnp.where(mask, item["system"], zero16)).astype(BF16)
+        for item in stage:
+            item["inverse"] = item["inverse"] + mm(item["step"], item["inv16"])
+    for item in stage:
+        right_hand = jnp.concatenate(
+            [item["values"][:PAIR], widened(item["left"] * item["half"], same)], axis=1
+        )
+        item["solved"] = mm(item["inverse"], right_hand).astype(BF16)
+    chunks = []
+    for item in stage:
+        half = item["half"]
+        seen = mm(item["read_rate"], item["solved"])
+        zero = item["values"][PAIR:] + seen[:, :PAIR]
+        reader = (widened(item["read"] * half, same) + seen[:, PAIR:]).astype(BF16)
+        wide_be = widened(item["b_side"] * half, same).astype(BF16)
+        wide_ke = widened(item["k_side"] * half, same).astype(BF16)
+        moved = mm_lt(item["solved"], wide_be)
+        update = moved[:PAIR] + mm_lt(item["wide_v"], wide_ke)
+        chunks.append((zero, reader, moved[PAIR:].astype(BF16), update, jnp.exp(item["total"])))
 
     carry = jnp.concatenate([eye, jnp.zeros((PAIR, PAIR), F32)], axis=0)
     for number, (zero, reader, change, update, fade) in enumerate(chunks):
@@ -271,6 +288,221 @@
         compiler_params=pltpu.CompilerParams(vmem_limit_bytes=48 * 1024 * 1024),
         name="wkv_finish",
     )(place, zero, reader, extra, glow, gsec, vec, state, *moved)
+
+
+MESH = pl.DeviceIdType.MESH
+
+
+def summed_kernel(
+    way, places, left_ref, right_ref, rest_ref, gain_ref, bias_ref,
+    out_ref, kept_ref, part_ref, acc_ref, recv_ref,
+    rs_send, rs_recv, ag_send, ag_recv,
+):
+    bits = places.bit_length() - 1
+    tokens, width = out_ref.shape
+    rows = tokens // places
+    wide = width // 2
+    me = lax.axis_index("tp")
+    mine = [(me // (1 << d)) % 2 for d in range(bits)]
+    partners = [me + (1 << d) * (1 - 2 * mine[d]) for d in range(bits)]
+    orders = [list(range(bits)), list(range(1)) + list(range(bits - 1, 0, -1))]
+    weight = [1 << (bits - 1 - d) for d in range(bits)]
+
+    def frees(order, step):
+        dims = order[step + 1 :]
+        for code in range(1 << len(dims)):
+            yield code, {d: (code >> n) % 2 for n, d in enumerate(dims)}
+
+    def block(free, flipped=None):
+        total = 0
+        for d in range(bits):
+            value = free[d] if d in free else (1 - mine[d] if d == flipped else mine[d])
+            total = total + value * weight[d]
+        return total
+
+    def area(at, side):
+        return pl.ds(pl.multiple_of(at * rows, rows), rows), pl.ds(side * wide, wide)
+
+    barrier = pltpu.get_barrier_semaphore()
+    for partner in partners:
+        pl.semaphore_signal(barrier, inc=1, device_id={"tp": partner}, device_id_type=MESH)
+    pl.semaphore_wait(barrier, bits)
+
+    def product(first, side):
+        group = pl.ds(pl.multiple_of(first * (tokens // 2), tokens // 2), tokens // 2)
+        tile = 512
+
+        def one(n, _):
+            cols = pl.ds(pl.multiple_of(side * wide + n * tile, tile), tile)
+            part_ref[group, cols] = jnp.dot(
+                left_ref[group, :], right_ref[:, cols], preferred_element_type=F32
+            ).astype(BF16)
+            return 0
+
+        lax.fori_loop(0, wide // tile, one, 0)
+
+    starts = [places - (1 << (bits - step)) for step in range(bits)]
+    sent = []
+
+    def scatter(side, step, code, free):
+        order = orders[side]
+        dim = order[step]
+        slot = starts[step] + code
+        at = block(free, dim)
+        source = part_ref.at[area(at, side)] if step == 0 else acc_ref.at[side, at]
+        copy = pltpu.make_async_remote_copy(
+            src_ref=source,
+            dst_ref=recv_ref.at[side, slot],
+            send_sem=rs_send.at[side, slot],
+            recv_sem=rs_recv.at[side, slot],
+            device_id={"tp": partners[dim]},
+            device_id_type=MESH,
+        )
+        copy.start()
+        sent.append(copy)
+
+    def gathered(side, step, code, free):
+        order = orders[side]
+        slot = starts[step] + code
+        at = block(free)
+        pltpu.make_async_remote_copy(
+            src_ref=recv_ref.at[side, slot],
+            dst_ref=recv_ref.at[side, slot],
+            send_sem=rs_send.at[side, slot],
+            recv_sem=rs_recv.at[side, slot],
+            device_id={"tp": partners[order[step]]},
+            device_id_type=MESH,
+        ).wait_recv()
+        base = pl.multiple_of(at * rows, rows)
+        tile = 16
+
+        def one(n, _):
+            here = pl.ds(pl.multiple_of(n * tile, tile), tile)
+            if step == 0:
+                there = pl.ds(pl.multiple_of(base + n * tile, tile), tile)
+                own = part_ref[there, pl.ds(side * wide, wide)]
+            else:
+                own = acc_ref[side, at, here, :]
+            acc_ref[side, at, here, :] = (
+                own.astype(F32) + recv_ref[side, slot, here, :].astype(F32)
+            ).astype(BF16)
+            return 0
+
+        lax.fori_loop(0, rows // tile, one, 0)
+
+    for side in range(2):
+        product(1 - mine[0], side)
+        for code, free in frees(orders[side], 0):
+            scatter(side, 0, code, free)
+    for side in range(2):
+        product(mine[0], side)
+    for step in range(bits):
+        for side in range(2):
+            for code, free in frees(orders[side], step):
+                gathered(side, step, code, free)
+            if step + 1 < bits:
+                for code, free in frees(orders[side], step + 1):
+                    scatter(side, step + 1, code, free)
+
+    here_block = block({})
+    base = pl.multiple_of(here_block * rows, rows)
+    tile = 16
+
+    def finish(n, _):
+        here = pl.ds(pl.multiple_of(n * tile, tile), tile)
+        there = pl.ds(pl.multiple_of(base + n * tile, tile), tile)
+        total = jnp.concatenate(
+            [acc_ref[0, here_block, here, :], acc_ref[1, here_block, here, :]], axis=1
+        ).astype(F32)
+        middle = (rest_ref[here, :].astype(F32) + total).astype(BF16)
+        if way == "norm":
+            kept_ref[here, :] = middle
+            floats = middle.astype(F32)
+            centered = floats - jnp.mean(floats, axis=-1, keepdims=True)
+            variance = jnp.mean(centered * centered, axis=-1, keepdims=True)
+            middle = (
+                centered * lax.rsqrt(variance + 1e-05) * gain_ref[...] + bias_ref[...]
+            ).astype(BF16)
+        out_ref[there, :] = middle
+        return 0
+
+    lax.fori_loop(0, rows // tile, finish, 0)
+    if way != "norm":
+        kept_ref[...] = jnp.zeros_like(kept_ref)
+
+    def share(side, step, at):
+        dim = orders[side][step]
+        copy = pltpu.make_async_remote_copy(
+            src_ref=out_ref.at[area(at, side)],
+            dst_ref=out_ref.at[area(at, side)],
+            send_sem=ag_send.at[side, step, at],
+            recv_sem=ag_recv.at[side, at],
+            device_id={"tp": partners[dim]},
+            device_id_type=MESH,
+        )
+        copy.start()
+        sent.append(copy)
+
+    for step in range(bits - 1, -1, -1):
+        for side in range(2):
+            share(side, step, here_block)
+    for step in range(bits - 1, -1, -1):
+        for side in range(2):
+            for code, free in frees(orders[side], step):
+                at = block(free, orders[side][step])
+                pltpu.make_async_remote_copy(
+                    src_ref=out_ref.at[area(at, side)],
+                    dst_ref=out_ref.at[area(at, side)],
+                    send_sem=ag_send.at[side, step, at],
+                    recv_sem=ag_recv.at[side, at],
+                    device_id={"tp": partners[orders[side][step]]},
+                    device_id_type=MESH,
+                ).wait_recv()
+                for later in range(step - 1, -1, -1):
+                    share(side, later, at)
+    for copy in sent:
+        copy.wait_send()
+
+
+def summed(way, number, left, right, rest, gain, bias):
+    places = lax.axis_size("tp")
+    bits = places.bit_length() - 1
+    tokens = left.shape[0]
+    width = right.shape[1]
+    rows = tokens // places
+    small = (rows, width) if way == "norm" else (8, 128)
+    vmem = pl.BlockSpec(memory_space=pltpu.VMEM)
+    return pl.pallas_call(
+        functools.partial(summed_kernel, way, places),
+        in_specs=[vmem] * 5,
+        out_specs=[vmem, vmem],
+        out_shape=[
+            jax.ShapeDtypeStruct((tokens, width), BF16),
+            jax.ShapeDtypeStruct(small, BF16),
+        ],
+        scratch_shapes=[
+            pltpu.VMEM((tokens, width), BF16),
+            pltpu.VMEM((2, places, rows, width // 2), BF16),
+            pltpu.VMEM((2, places - 1, rows, width // 2), BF16),
+            pltpu.SemaphoreType.DMA((2, places - 1)),
+            pltpu.SemaphoreType.DMA((2, places - 1)),
+            pltpu.SemaphoreType.DMA((2, bits, places)),
+            pltpu.SemaphoreType.DMA((2, places)),
+        ],
+        compiler_params=pltpu.CompilerParams(
+            collective_id=number, has_side_effects=True, vmem_limit_bytes=56 * 1024 * 1024
+        ),
+        name="summed_" + way,
+    )(left, right, rest, gain.reshape(1, -1), bias.reshape(1, -1))
+
+
+def own_rows(matrix):
+    places = lax.axis_size("tp")
+    bits = places.bit_length() - 1
+    me = lax.axis_index("tp")
+    place = sum(((me // (1 << d)) % 2) * (1 << (bits - 1 - d)) for d in range(bits))
+    rows = matrix.shape[0] // places
+    return lax.dynamic_slice_in_dim(matrix, place * rows, rows, axis=0)
 
 
 def shards(
@@ -349,14 +581,10 @@
         head_state_initial,
         arrivals,
     )
-    attended = lax.psum(
-        jnp.dot(lagged_embedding, time_output_weight, preferred_element_type=jnp.float32).astype(
-            jnp.bfloat16
-        ),
-        "tp",
-    ).astype(jnp.float32)
-    middle = (stream.astype(jnp.float32) + attended).astype(jnp.bfloat16)
-    normed_next = layer_norm(middle, channel_norm_gain, channel_norm_bias)
+    normed_next, middle = summed(
+        "norm", 0, lagged_embedding, time_output_weight, own_rows(stream),
+        channel_norm_gain, channel_norm_bias,
+    )
     arrived_next = passed_along(normed_next[-1:], "ctx", 1)
     previous_next = jnp.concatenate(
         [jnp.where(ctx_first, channel_previous_token[None, :], arrived_next), normed_next[:-1]],
@@ -367,13 +595,9 @@
         jnp.dot(channel_in, channel_key_weight, preferred_element_type=jnp.float32), 0.0
     )
     hidden = (expanded * expanded).astype(jnp.bfloat16)
-    channel = lax.psum(
-        jnp.dot(hidden, channel_value_weight, preferred_element_type=jnp.float32).astype(
-            jnp.bfloat16
-        ),
-        "tp",
-    ).astype(jnp.float32)
-    layer_out = (middle.astype(jnp.float32) + channel).astype(jnp.bfloat16)
+    layer_out, _ = summed(
+        "plain", 1, hidden, channel_value_weight, middle, channel_norm_gain, channel_norm_bias
+    )
     return layer_out
 
 

time: 335 us -> 206 us (0.61)
  waiting for transfers between devices: 169 us -> 1.99 us
  Pallas kernels: 68.2 us -> 133 us
  other arithmetic: 25 us -> 6.63 us
  between operations: 14 us -> 0.58 us
  local copies, waits for them, and re-layouts: 2.26 us -> 11.2 us
  matrix products: 37.5 us -> 30.4 us
    psum x2 -> x0, waiting for transfers between devices: 166 us -> none  [the longest x1 84.5 us: shards(): lax.psum(jnp.dot(lagged_embedding, time_output_weight, preferred_element_...]
    pallas_call x0 -> x2, Pallas kernels: none -> 107 us  [summed(): pl.pallas_call(functools.partial(summed_kernel, way, places), in_specs=[v...]
    pallas_call x1, Pallas kernels: 63.3 us -> 20.4 us  [wkv_local(): pl.pallas_call(local_kernel, grid=(count,), in_specs=[by_pair, by_pair, b...]
    dot_general x2 -> x0, matrix products: 13.8 us -> none  [the longest x1 9.48 us: shards(): jnp.dot(hidden, channel_value_weight, preferred_element_type=jnp.float32)]
    convert_element_type x1 -> x0, other arithmetic: 7.25 us -> none  [shards(): layer_out = (middle.astype(jnp.float32) + channel).astype(jnp.bfloat16)]
    dot_general x1, matrix products: 4.74 us -> 11.4 us  [shards(): jnp.dot(channel_in, channel_key_weight, preferred_element_type=jnp.float32)]
    unnamed x66 -> x57, local copies, waits for them, and re-layouts: 2.18 us -> 8.41 us
    reduce_sum x2 -> x1, other arithmetic: 8.29 us -> 2.96 us  [layer_norm(): average = jnp.mean(floats, axis=-1, keepdims=True)]
  transfers between devices with their start and end apart: 7 -> 5, of which waited for: 5 -> 2; matrix products, arithmetic and copies ran while one was open for 1% -> 2% of each run, Pallas kernels for 0% -> 0%
where the time goes in v2:
time: 206 us; the launch traced here: 204 us
  Pallas kernels  133 us (65%)
  matrix products  30.4 us (15%)
  starting transfers between devices  20.4 us (10%)
  local copies, waits for them, and re-layouts  11.2 us (5%)
  other arithmetic  6.63 us (3%)
    pallas_call x2, Pallas kernels, summed(): pl.pallas_call(functools.partial(summed_kernel, way, places), in_specs=[v...  107 us
    pallas_call x1, Pallas kernels, wkv_local(): pl.pallas_call(local_kernel, grid=(count,), in_specs=[by_pair, by_pair, b...  20.4 us
    ppermute x5, starting transfers between devices, passed_along(): return lax.ppermute(shard, axis, pairs)  20.4 us
    dot_general x1, matrix products, shards(): jnp.dot(channel_in, channel_key_weight, preferred_element_type=jnp.float32)  11.4 us
    unnamed x57, local copies, waits for them, and re-layouts  8.41 us
    dot_general x1, matrix products, shards(): jnp.dot(inputs[4], rate_first_factor, preferred_element_type=F32)  5.82 us
    pallas_call x1, Pallas kernels, wkv_finish(): pl.pallas_call(finish_kernel, grid=(count,), in_specs=[pl.BlockSpec(memor...  4.89 us
  transfers between devices with their start and end apart: 5, of which 2 were waited for; matrix products, arithmetic and copies ran while one was open for 2% of the time, Pallas kernels for 0%

profile of v2, /device:TPU:0, one launch (start us, length us, event | category | flops | bytes accessed | tf_op | source)
XLA Modules:
  0.0 204.0 jit_solution(5544732742041354190)
XLA Ops:
  0.0 3.0 %convert_reduce_fusion = f32[512]{0:T(512)S(1)} fusion(bf16[512,4096]{1,0:T(8,128)(2,1)} %param.29), kind=kLoop, calls=%fused_computation.10 | loop fusion | flops 4193792 | bytes 4196352 | tf_op jit(solution)/shard_map/reduce_sum | solution.py:25
  3.6 1.2 fusion.2
  5.0 2.3 %fusion.5 = bf16[512,4096]{1,0:T(8,128)(2,1)S(1)} fusion(bf16[512,4096]{1,0:T(8,128)(2,1)S(1)} %copy-done.7, f32[4096]{0:T(1024)S(1)} %copy-done.11, f32[4096]{0:T(1024)S(1)} %copy-done.12, f32[512]{0:T(512)S(1)} %add_rsqrt_fusion, f32[512]{0:T(512)S(1)} %broadcast_multiply_fusion), kind=kLoop, calls=%fused_computation.16 | loop fusion | flops 12582912 | bytes 8425472 | tf_op jit(solution)/shard_map/convert_element_type | solution.py:28
  7.3 2.0 copy-done.8
  9.3 5.1 %collective-permute-start = (bf16[1,4096]{1,0:T(2,128)(2,1)S(1)}, bf16[1,4096]{1,0:T(2,128)(2,1)S(1)}, u32[]{:S(2)}, u32[]{:S(2)}) collective-permute-start(bf16[1,4096]{1,0:T(2,128)(2,1)S(1)} %slice.40), channel_id=1, source_target_pairs={{0,8},{8,16},{16,24},{1,9},{9,17},{17,25},{2,10},{10,18},{18,26},{... | collective-permute-start | bytes 24584 | tf_op jit(solution)/shard_map/ppermute | solution.py:20
  14.6 1.9 constant_dynamic-slice_fusion.rest_ref
  16.7 5.8 %fusion.68.rlow_ref = bf16[512,128]{1,0:T(8,128)(2,1)S(1)} fusion(bf16[4096,128]{1,0:T(8,128)(2,1)S(1)} %copy-done.26, bf16[512,4096]{1,0:T(8,128)(2,1)} %copy-done.8, f32[4096]{0:T(1024)S(1)} %bitcast.40, bf16[511,4096]{1,0:T(8,128)(2,1)} %bitcast.25, bf16[1,4096]{1,0:T(2,128)(2,1)S(1)} %broadcast_select_fusion.1), kind=kOutput, calls=%fused_computation.52 | convolution fusion | flops 555810816 | bytes 9584640 | tf_op jit(solution)/shard_map/dot_general | solution.py:553
  22.6 3.0 %fusion.65.dlow_ref = bf16[512,128]{1,0:T(8,128)(2,1)S(1)} fusion(bf16[4096,128]{1,0:T(8,128)(2,1)S(1)} %copy-done.27, bf16[512,4096]{1,0:T(8,128)(2,1)S(1)} %copy-done.9, f32[4096]{0:T(1024)S(1)} %bitcast.39, bf16[511,4096]{1,0:T(8,128)(2,1)S(1)} %bitcast.26, bf16[1,4096]{1,0:T(2,128)(2,1)S(1)} %broadcast_select_fusion.1), kind=kOutput, calls=%fused_computation.51 | convolution fusion | flops 555810816 | bytes 9584640 | tf_op jit(solution)/shard_map/dot_general | solution.py:551
  25.6 2.4 %fusion.44.value_ref = bf16[512,512]{1,0:T(8,128)(2,1)S(1)} fusion(bf16[4096,512]{1,0:T(8,128)(2,1)S(1)} %copy-done.23, bf16[512,4096]{1,0:T(8,128)(2,1)S(1)} %copy-done.9, f32[4096]{0:T(1024)S(1)} %bitcast.38, bf16[511,4096]{1,0:T(8,128)(2,1)S(1)} %bitcast.27, bf16[1,4096]{1,0:T(2,128)(2,1)S(1)} %broadcast_select_fusion.1), kind=kOutput, calls=%fused_computation.44 | convolution fusion | flops 2166620160 | bytes 13123584 | tf_op jit(solution)/shard_map/dot_general | solution.py:549
  28.0 2.5 %fusion.41.key_ref = bf16[512,512]{1,0:T(8,128)(2,1)S(1)} fusion(bf16[4096,512]{1,0:T(8,128)(2,1)S(1)} %copy-done.24, bf16[512,4096]{1,0:T(8,128)(2,1)S(1)} %copy-done.9, f32[4096]{0:T(1024)S(1)} %bitcast.37, bf16[511,4096]{1,0:T(8,128)(2,1)S(1)} %bitcast.28, bf16[1,4096]{1,0:T(2,128)(2,1)S(1)} %broadcast_select_fusion.1), kind=kOutput, calls=%fused_computation.43 | convolution fusion | flops 2166620160 | bytes 13123584 | tf_op jit(solution)/shard_map/dot_general | solution.py:548
  30.5 2.5 %fusion.38.recept_ref = bf16[512,512]{1,0:T(8,128)(2,1)S(1)} fusion(bf16[4096,512]{1,0:T(8,128)(2,1)S(1)} %copy-done.25, bf16[512,4096]{1,0:T(8,128)(2,1)S(1)} %copy-done.9, f32[4096]{0:T(1024)S(1)} %bitcast.36, bf16[511,4096]{1,0:T(8,128)(2,1)S(1)} %bitcast.29, bf16[1,4096]{1,0:T(2,128)(2,1)S(1)} %broadcast_select_fusion.1), kind=kOutput, calls=%fused_computation.42 | convolution fusion | flops 2166620160 | bytes 13123584 | tf_op jit(solution)/shard_map/dot_general | solution.py:547
  33.0 20.4 %wkv_local.1 = (f32[512,512]{1,0:T(8,128)S(1)}, bf16[512,512]{1,0:T(8,128)(2,1)S(1)}, f32[512,512]{1,0:T(8,128)S(1)}, bf16[4,2,64,128]{3,2,1,0:T(8,128)(2,1)S(1)}) custom-call(bf16[512,512]{1,0:T(8,128)(2,1)S(1)} %fusion.38.recept_ref, bf16[512,512]{1,0:T(8,128)(2,1)S(1)} %fusion.41.key_ref, bf16[512,512]{1,0:T(8,128)(2,1)S(1)} %fusion.44.value_ref, ...), custom_call_target="tpu_custom_call" | custom-call | tf_op jit(solution)/shard_map/wkv_local/pallas_call | solution.py:216
  53.4 5.3 %collective-permute-start.3 = (bf16[4,2,64,128]{3,2,1,0:T(8,128)(2,1)S(1)}, bf16[4,2,64,128]{3,2,1,0:T(8,128)(2,1)S(1)}, u32[]{:S(2)}, u32[]{:S(2)}) collective-permute-start(bf16[4,2,64,128]{3,2,1,0:T(8,128)(2,1)S(1)} %get-tuple-element.15), channel_id=1, source_target_pairs={{0,24},{1,25},{2,26},{3,27},{4,28},{5,29},{6,30},{7,31}} | collective-permute-start | bytes 393224 | tf_op jit(solution)/shard_map/ppermute | solution.py:20
  58.7 1.3 collective-permute-start.2
  60.0 2.5 %collective-permute-start.1 = (bf16[4,2,64,128]{3,2,1,0:T(8,128)(2,1)S(1)}, bf16[4,2,64,128]{3,2,1,0:T(8,128)(2,1)S(1)}, u32[]{:S(2)}, u32[]{:S(2)}) collective-permute-start(bf16[4,2,64,128]{3,2,1,0:T(8,128)(2,1)S(1)} %get-tuple-element.15), channel_id=1, source_target_pairs={{0,8},{8,16},{16,24},{1,9},{9,17},{17,25},{2,10},{10,18},{18,26},{... | collective-permute-start | bytes 393224 | tf_op jit(solution)/shard_map/ppermute | solution.py:20
  62.6 2.8 %fusion.59.glow_ref = bf16[512,256]{1,0:T(8,128)(2,1)S(1)} fusion(bf16[4096,256]{1,0:T(8,128)(2,1)S(1)} %copy-done, bf16[512,4096]{1,0:T(8,128)(2,1)S(1)} %copy-done.9, f32[4096]{0:T(1024)S(1)} %bitcast.35, bf16[511,4096]{1,0:T(8,128)(2,1)S(1)} %bitcast.30, bf16[1,4096]{1,0:T(2,128)(2,1)S(1)} %broadcast_select_fusion.1), kind=kOutput, calls=%fused_computation.49 | convolution fusion | flops 1093140480 | bytes 10764288 | tf_op jit(solution)/shard_map/dot_general | solution.py:555
  66.0 4.9 %wkv_finish.1.left_ref = bf16[512,512]{1,0:T(8,128)(2,1)S(1)} custom-call(s32[1]{0:T(128)} %bitcast.place_ref, f32[512,512]{1,0:T(8,128)S(1)} %get-tuple-element.12.zero_ref, bf16[512,512]{1,0:T(8,128)(2,1)S(1)} %get-tuple-element.13.reader_ref, f32[512,512]{1,0:T(8,128)S(1)} %get-tuple-element.14.extra_ref, bf16[512,256]{1,0:T(8,128)(2,1)S(1)} %fusion.59.glow_ref, ...), custom_call_target="tpu_custom_call" | custom-call | tf_op jit(solution)/shard_map/wkv_finish/pallas_call | solution.py:272
  71.7 53.5 %summed_norm.1 = (bf16[512,4096]{1,0:T(8,128)(2,1)}, bf16[64,4096]{1,0:T(8,128)(2,1)}) custom-call(bf16[512,512]{1,0:T(8,128)(2,1)} %copy-done.2, bf16[512,4096]{1,0:T(8,128)(2,1)} %right_ref.2, bf16[64,4096]{1,0:T(8,128)(2,1)} %constant_dynamic-slice_fusion.rest_ref, f32[1,4096]{1,0:T(1,128)} %bitcast.31, f32[1,4096]{1,0:T(1,128)} %bitcast.33), custom_call_target="tpu_custom_call" | custom-call | tf_op jit(solution)/shard_map/summed_norm/pallas_call | solution.py:475
  125.2 0.9 slice.38
  126.0 6.2 %collective-permute-start.4 = (bf16[1,4096]{1,0:T(2,128)(2,1)S(1)}, bf16[1,4096]{1,0:T(2,128)(2,1)S(1)}, u32[]{:S(2)}, u32[]{:S(2)}) collective-permute-start(bf16[1,4096]{1,0:T(2,128)(2,1)S(1)} %slice.38), channel_id=1, source_target_pairs={{0,8},{8,16},{16,24},{1,9},{9,17},{17,25},{2,10},{10,18},{18,26},{... | collective-permute-start | bytes 24584 | tf_op jit(solution)/shard_map/ppermute | solution.py:20
  132.2 1.4 collective-permute-done.4
  133.7 11.4 %multiply_convert_fusion.left_ref = bf16[512,1024]{1,0:T(8,128)(2,1)} fusion(bf16[4096,1024]{1,0:T(8,128)(2,1)} %param.56, bf16[512,4096]{1,0:T(8,128)(2,1)} %get-tuple-element.16, bf16[511,4096]{1,0:T(8,128)(2,1)} %bitcast.49, bf16[1,4096]{1,0:T(2,128)(2,1)S(1)} %broadcast_select_fusion, f32[4096]{0:T(1024)S(1)} %convert_element_type.103), kind=kOutput, calls=%fused_computation.41 | convolution fusion | flops 4315414528 | bytes 17842176 | tf_op jit(solution)/shard_map/dot_general | solution.py:595
  145.1 54.0 %summed_plain.1 = (bf16[512,4096]{1,0:T(8,128)(2,1)}, bf16[8,128]{1,0:T(8,128)(2,1)}) custom-call(bf16[512,1024]{1,0:T(8,128)(2,1)} %multiply_convert_fusion.left_ref, bf16[1024,4096]{1,0:T(8,128)(2,1)} %right_ref.3, bf16[64,4096]{1,0:T(8,128)(2,1)} %get-tuple-element.17.rest_ref, f32[1,4096]{1,0:T(1,128)} %bitcast.32, f32[1,4096]{1,0:T(1,128)} %bitcast.34), custom_call_target="tpu_custom_call" | custom-call | tf_op jit(solution)/shard_map/summed_plain/pallas_call | solution.py:475
  199.1 4.8 %copy.31 = bf16[512,4096]{1,0:T(8,128)(2,1)} copy(bf16[512,4096]{1,0:T(8,128)(2,1)} %get-tuple-element.18) | data formatting | bytes 8388608
  (67 shorter events, 2.3 us)
Async XLA Ops:
  0.0 62.5 %copy-start = (bf16[4096,256]{1,0:T(8,128)(2,1)S(1)}, bf16[4096,256]{1,0:T(8,128)(2,1)}, u32[]{:S(2)}) copy-start(bf16[4096,256]{1,0:T(8,128)(2,1)} %param.45) | copy-start | bytes 6291460
  0.0 3.6 %copy-start.7 = (bf16[512,4096]{1,0:T(8,128)(2,1)S(1)}, bf16[512,4096]{1,0:T(8,128)(2,1)}, u32[]{:S(2)}) copy-start(bf16[512,4096]{1,0:T(8,128)(2,1)} %param.29) | copy-start | bytes 12582916
  0.0 4.8 %copy-start.11 = (f32[4096]{0:T(1024)S(1)}, f32[4096]{0:T(1024)}, u32[]{:S(2)}) copy-start(f32[4096]{0:T(1024)} %param.34) | copy-start | bytes 49156
  0.0 4.8 %copy-start.12 = (f32[4096]{0:T(1024)S(1)}, f32[4096]{0:T(1024)}, u32[]{:S(2)}) copy-start(f32[4096]{0:T(1024)} %param.33) | copy-start | bytes 49156
  4.9 9.7 %copy-start.10 = (bf16[6,4096]{1,0:T(8,128)(2,1)S(1)}, bf16[6,4096]{1,0:T(8,128)(2,1)}, u32[]{:S(2)}) copy-start(bf16[6,4096]{1,0:T(8,128)(2,1)} %param.35) | copy-start | bytes 147460
  4.9 11.7 %copy-start.14 = (f32[512]{0:T(512)S(1)}, f32[512]{0:T(512)}, u32[]{:S(2)}) copy-start(f32[512]{0:T(512)} %param.51) | copy-start | bytes 6148
  4.9 11.7 %copy-start.17 = (f32[512]{0:T(512)S(1)}, f32[512]{0:T(512)}, u32[]{:S(2)}) copy-start(f32[512]{0:T(512)} %param.41) | copy-start | bytes 6148
  4.9 11.7 %copy-start.18 = (f32[512]{0:T(512)S(1)}, f32[512]{0:T(512)}, u32[]{:S(2)}) copy-start(f32[512]{0:T(512)} %param.44) | copy-start | bytes 6148
  4.9 11.6 %copy-start.19 = (f32[512]{0:T(512)S(1)}, f32[512]{0:T(512)}, u32[]{:S(2)}) copy-start(f32[512]{0:T(512)} %param.47) | copy-start | bytes 6148
  4.9 11.6 %copy-start.20 = (f32[512]{0:T(512)S(1)}, f32[512]{0:T(512)}, u32[]{:S(2)}) copy-start(f32[512]{0:T(512)} %param.48) | copy-start | bytes 6148
  4.9 11.6 %copy-start.21 = (f32[512]{0:T(512)S(1)}, f32[512]{0:T(512)}, u32[]{:S(2)}) copy-start(f32[512]{0:T(512)} %param.49) | copy-start | bytes 6148
  4.9 11.6 %copy-start.22 = (f32[512]{0:T(512)S(1)}, f32[512]{0:T(512)}, u32[]{:S(2)}) copy-start(f32[512]{0:T(512)} %param.50) | copy-start | bytes 6148
  5.0 11.7 %copy-start.15 = (bf16[4096]{0:T(1024)(128)(2,1)S(1)}, bf16[4096]{0:T(1024)(128)(2,1)}, u32[]{:S(2)}) copy-start(bf16[4096]{0:T(1024)(128)(2,1)} %param.30) | copy-start | bytes 24580
  5.0 11.7 %copy-start.26 = (bf16[4096,128]{1,0:T(8,128)(2,1)S(1)}, bf16[4096,128]{1,0:T(8,128)(2,1)}, u32[]{:S(2)}) copy-start(bf16[4096,128]{1,0:T(8,128)(2,1)} %param.42) | copy-start | bytes 3145732
  9.3 7.3 %collective-permute-start = (bf16[1,4096]{1,0:T(2,128)(2,1)S(1)}, bf16[1,4096]{1,0:T(2,128)(2,1)S(1)}, u32[]{:S(2)}, u32[]{:S(2)}) collective-permute-start(bf16[1,4096]{1,0:T(2,128)(2,1)S(1)} %slice.40), channel_id=1, source_target_pairs={{0,8},{8,16},{16,24},{1,9},{9,17},{17,25},{2,10},{10,18},{18,26},{... | collective-permute-start | bytes 24584 | tf_op jit(solution)/shard_map/ppermute | solution.py:20
  16.7 5.8 %copy-start.9 = (bf16[512,4096]{1,0:T(8,128)(2,1)S(1)}, bf16[512,4096]{1,0:T(8,128)(2,1)}, u32[]{:S(2)}) copy-start(bf16[512,4096]{1,0:T(8,128)(2,1)} %copy-done.8) | copy-start | bytes 12582916
  16.7 5.8 %copy-start.27 = (bf16[4096,128]{1,0:T(8,128)(2,1)S(1)}, bf16[4096,128]{1,0:T(8,128)(2,1)}, u32[]{:S(2)}) copy-start(bf16[4096,128]{1,0:T(8,128)(2,1)} %param.39) | copy-start | bytes 3145732
  53.4 12.0 %collective-permute-start.3 = (bf16[4,2,64,128]{3,2,1,0:T(8,128)(2,1)S(1)}, bf16[4,2,64,128]{3,2,1,0:T(8,128)(2,1)S(1)}, u32[]{:S(2)}, u32[]{:S(2)}) collective-permute-start(bf16[4,2,64,128]{3,2,1,0:T(8,128)(2,1)S(1)} %get-tuple-element.15), channel_id=1, source_target_pairs={{0,24},{1,25},{2,26},{3,27},{4,28},{5,29},{6,30},{7,31}} | collective-permute-start | bytes 393224 | tf_op jit(solution)/shard_map/ppermute | solution.py:20
  58.7 6.7 %collective-permute-start.2 = (bf16[4,2,64,128]{3,2,1,0:T(8,128)(2,1)S(1)}, bf16[4,2,64,128]{3,2,1,0:T(8,128)(2,1)S(1)}, u32[]{:S(2)}, u32[]{:S(2)}) collective-permute-start(bf16[4,2,64,128]{3,2,1,0:T(8,128)(2,1)S(1)} %get-tuple-element.15), channel_id=1, source_target_pairs={{0,16},{8,24},{1,17},{9,25},{2,18},{10,26},{3,19},{11,27},{4,20},{... | collective-permute-start | bytes 393224 | tf_op jit(solution)/shard_map/ppermute | solution.py:20
  60.0 6.0 %collective-permute-start.1 = (bf16[4,2,64,128]{3,2,1,0:T(8,128)(2,1)S(1)}, bf16[4,2,64,128]{3,2,1,0:T(8,128)(2,1)S(1)}, u32[]{:S(2)}, u32[]{:S(2)}) collective-permute-start(bf16[4,2,64,128]{3,2,1,0:T(8,128)(2,1)S(1)} %get-tuple-element.15), channel_id=1, source_target_pairs={{0,8},{8,16},{16,24},{1,9},{9,17},{17,25},{2,10},{10,18},{18,26},{... | collective-permute-start | bytes 393224 | tf_op jit(solution)/shard_map/ppermute | solution.py:20
  66.0 66.2 %copy-start.13 = (bf16[4096]{0:T(1024)(128)(2,1)S(1)}, bf16[4096]{0:T(1024)(128)(2,1)}, u32[]{:S(2)}) copy-start(bf16[4096]{0:T(1024)(128)(2,1)} %param.55) | copy-start | bytes 24580
  66.0 67.6 %copy-start.16 = (bf16[4096]{0:T(1024)(128)(2,1)S(1)}, bf16[4096]{0:T(1024)(128)(2,1)}, u32[]{:S(2)}) copy-start(bf16[4096]{0:T(1024)(128)(2,1)} %param.31) | copy-start | bytes 24580
  126.0 7.6 %collective-permute-start.4 = (bf16[1,4096]{1,0:T(2,128)(2,1)S(1)}, bf16[1,4096]{1,0:T(2,128)(2,1)S(1)}, u32[]{:S(2)}, u32[]{:S(2)}) collective-permute-start(bf16[1,4096]{1,0:T(2,128)(2,1)S(1)} %slice.38), channel_id=1, source_target_pairs={{0,8},{8,16},{16,24},{1,9},{9,17},{17,25},{2,10},{10,18},{18,26},{... | collective-permute-start | bytes 24584 | tf_op jit(solution)/shard_map/ppermute | solution.py:20
  199.1 4.9 %copy-start.1 = (bf16[4096,256]{1,0:T(8,128)(2,1)S(1)}, bf16[4096,256]{1,0:T(8,128)(2,1)}, u32[]{:S(2)}) copy-start(bf16[4096,256]{1,0:T(8,128)(2,1)} %param.45) | copy-start | bytes 6291460
  (9 other events, 22.6 us)

commit v3 on v2

--- a/solution.py
+++ b/solution.py
@@ -207,16 +207,19 @@
     moved_ref[0, 1] = folded(carry[PAIR:]).astype(BF16)
 
 
-def wkv_local(recept, keys, values, dlow, rlow, dsec, rsec, vec):
-    tokens, width = recept.shape
-    count = width // PAIR
+def wkv_local(half, recept, keys, values, dlow, rlow, dsec, rsec, vec):
+    tokens = recept.shape[0]
+    count = recept.shape[1] // PAIR // 2
+    width = count * PAIR
+    base = half * count
     by_pair = pl.BlockSpec((tokens, PAIR), lambda p: (0, p))
+    picked = pl.BlockSpec((tokens, PAIR), lambda p: (0, p + base))
     whole = lambda a: pl.BlockSpec(a.shape, lambda p: (0, 0))
-    cols = lambda a: pl.BlockSpec((a.shape[0], PAIR), lambda p: (0, p))
+    cols = lambda a: pl.BlockSpec((a.shape[0], PAIR), lambda p: (0, p + base))
     return pl.pallas_call(
         local_kernel,
         grid=(count,),
-        in_specs=[by_pair, by_pair, by_pair, whole(dlow), whole(rlow), cols(dsec), cols(rsec), cols(vec)],
+        in_specs=[picked, picked, picked, whole(dlow), whole(rlow), cols(dsec), cols(rsec), cols(vec)],
         out_specs=[
             by_pair,
             by_pair,
@@ -231,6 +234,9 @@
         ],
         scratch_shapes=[pltpu.VMEM((tokens, PAIR), F32)] * 4,
         compiler_params=pltpu.CompilerParams(vmem_limit_bytes=48 * 1024 * 1024),
+        cost_estimate=pl.CostEstimate(
+            flops=tokens * width * 4096, bytes_accessed=tokens * width * 20, transcendentals=tokens * width * 8
+        ),
         name="wkv_local",
     )(recept, keys, values, dlow, rlow, dsec, rsec, vec)
 
@@ -263,12 +269,13 @@
     out_ref[...] = ((normal + extra_ref[...]) * gate).astype(BF16)
 
 
-def wkv_finish(place, zero, reader, extra, glow, gsec, vec, state, moved):
+def wkv_finish(half, place, zero, reader, extra, glow, gsec, vec, state, moved):
     tokens, width = zero.shape
     count = width // PAIR
+    base = half * count
     by_pair = pl.BlockSpec((tokens, PAIR), lambda p: (0, p))
     whole = lambda a: pl.BlockSpec(a.shape, lambda p: (0, 0))
-    cols = lambda a: pl.BlockSpec((a.shape[0], PAIR), lambda p: (0, p))
+    cols = lambda a: pl.BlockSpec((a.shape[0], PAIR), lambda p: (0, p + base))
     return pl.pallas_call(
         finish_kernel,
         grid=(count,),
@@ -280,12 +287,15 @@
             whole(glow),
             cols(gsec),
             cols(vec),
-            pl.BlockSpec((2, LANE_SPAN, LANE_SPAN), lambda p: (p, 0, 0)),
+            pl.BlockSpec((2, LANE_SPAN, LANE_SPAN), lambda p: (p + base, 0, 0)),
         ]
         + [pl.BlockSpec((1, 2, LANE_SPAN, PAIR), lambda p: (p, 0, 0, 0))] * len(moved),
         out_specs=by_pair,
         out_shape=jax.ShapeDtypeStruct((tokens, width), BF16),
         compiler_params=pltpu.CompilerParams(vmem_limit_bytes=48 * 1024 * 1024),
+        cost_estimate=pl.CostEstimate(
+            flops=tokens * width * 1024, bytes_accessed=tokens * width * 14, transcendentals=tokens * width
+        ),
         name="wkv_finish",
     )(place, zero, reader, extra, glow, gsec, vec, state, *moved)
 
@@ -294,18 +304,22 @@
 
 
 def summed_kernel(
-    way, places, left_ref, right_ref, rest_ref, gain_ref, bias_ref,
-    out_ref, kept_ref, part_ref, acc_ref, recv_ref,
-    rs_send, rs_recv, ag_send, ag_recv,
+    way, places, count, *refs
 ):
+    left_refs = refs[:count]
+    (
+        right_ref, rest_ref, gain_ref, bias_ref, out_ref, kept_ref, last_ref,
+        part_ref, acc_ref, recv_ref, rs_send, rs_recv, ag_send, ag_recv, row_sem,
+    ) = refs[count:]
     bits = places.bit_length() - 1
     tokens, width = out_ref.shape
     rows = tokens // places
-    wide = width // 2
+    parts = acc_ref.shape[0]
+    wide = width // parts
     me = lax.axis_index("tp")
     mine = [(me // (1 << d)) % 2 for d in range(bits)]
     partners = [me + (1 << d) * (1 - 2 * mine[d]) for d in range(bits)]
-    orders = [list(range(bits)), list(range(1)) + list(range(bits - 1, 0, -1))]
+    orders = [list(range(bits)), list(range(1)) + list(range(bits - 1, 0, -1))] * (parts // 2)
     weight = [1 << (bits - 1 - d) for d in range(bits)]
 
     def frees(order, step):
@@ -326,16 +340,30 @@
     barrier = pltpu.get_barrier_semaphore()
     for partner in partners:
         pl.semaphore_signal(barrier, inc=1, device_id={"tp": partner}, device_id_type=MESH)
-    pl.semaphore_wait(barrier, bits)
+    if way == "norm":
+        blocks = lax.axis_size("ctx")
+        place = lax.axis_index("ctx")
+        after = lax.rem(place + 1, blocks)
+        for other in (after, lax.rem(place + blocks - 1, blocks)):
+            pl.semaphore_signal(barrier, inc=1, device_id={"ctx": other}, device_id_type=MESH)
+        pl.semaphore_wait(barrier, bits + 2)
+    else:
+        pl.semaphore_wait(barrier, bits)
 
     def product(first, side):
         group = pl.ds(pl.multiple_of(first * (tokens // 2), tokens // 2), tokens // 2)
         tile = 512
 
-        def one(n, _):
-            cols = pl.ds(pl.multiple_of(side * wide + n * tile, tile), tile)
-            part_ref[group, cols] = jnp.dot(
-                left_ref[group, :], right_ref[:, cols], preferred_element_type=F32
+        def one(tile_number, _):
+            cols = pl.ds(pl.multiple_of(side * wide + tile_number * tile, tile), tile)
+            depth = right_ref.shape[0] // count
+            part_ref[group, cols] = sum(
+                jnp.dot(
+                    left_refs[n][group, :],
+                    right_ref[n * depth : (n + 1) * depth, cols],
+                    preferred_element_type=F32,
+                )
+                for n in range(count)
             ).astype(BF16)
             return 0
 
@@ -390,14 +418,14 @@
 
         lax.fori_loop(0, rows // tile, one, 0)
 
-    for side in range(2):
+    for side in range(parts):
         product(1 - mine[0], side)
         for code, free in frees(orders[side], 0):
             scatter(side, 0, code, free)
-    for side in range(2):
-        product(mine[0], side)
     for step in range(bits):
-        for side in range(2):
+        for side in range(parts):
+            if step == 0:
+                product(mine[0], side)
             for code, free in frees(orders[side], step):
                 gathered(side, step, code, free)
             if step + 1 < bits:
@@ -412,7 +440,7 @@
         here = pl.ds(pl.multiple_of(n * tile, tile), tile)
         there = pl.ds(pl.multiple_of(base + n * tile, tile), tile)
         total = jnp.concatenate(
-            [acc_ref[0, here_block, here, :], acc_ref[1, here_block, here, :]], axis=1
+            [acc_ref[side, here_block, here, :] for side in range(parts)], axis=1
         ).astype(F32)
         middle = (rest_ref[here, :].astype(F32) + total).astype(BF16)
         if way == "norm":
@@ -429,6 +457,7 @@
     lax.fori_loop(0, rows // tile, finish, 0)
     if way != "norm":
         kept_ref[...] = jnp.zeros_like(kept_ref)
+        last_ref[...] = jnp.zeros_like(last_ref)
 
     def share(side, step, at):
         dim = orders[side][step]
@@ -444,10 +473,10 @@
         sent.append(copy)
 
     for step in range(bits - 1, -1, -1):
-        for side in range(2):
+        for side in range(parts):
             share(side, step, here_block)
     for step in range(bits - 1, -1, -1):
-        for side in range(2):
+        for side in range(parts):
             for code, free in frees(orders[side], step):
                 at = block(free, orders[side][step])
                 pltpu.make_async_remote_copy(
@@ -460,40 +489,57 @@
                 ).wait_recv()
                 for later in range(step - 1, -1, -1):
                     share(side, later, at)
+    if way == "norm":
+        copy = pltpu.make_async_remote_copy(
+            src_ref=out_ref.at[pl.ds(tokens - 16, 16), :],
+            dst_ref=last_ref,
+            send_sem=row_sem.at[0],
+            recv_sem=row_sem.at[1],
+            device_id={"ctx": after},
+            device_id_type=MESH,
+        )
+        copy.start()
+        copy.wait_recv()
+        sent.append(copy)
     for copy in sent:
         copy.wait_send()
 
 
 def summed(way, number, left, right, rest, gain, bias):
+    parts = 4
     places = lax.axis_size("tp")
     bits = places.bit_length() - 1
-    tokens = left.shape[0]
+    tokens = rest.shape[0] * places
     width = right.shape[1]
     rows = tokens // places
     small = (rows, width) if way == "norm" else (8, 128)
     vmem = pl.BlockSpec(memory_space=pltpu.VMEM)
+    left_specs = [vmem] * len(left)
+    lefts = left
     return pl.pallas_call(
-        functools.partial(summed_kernel, way, places),
-        in_specs=[vmem] * 5,
-        out_specs=[vmem, vmem],
+        functools.partial(summed_kernel, way, places, len(left)),
+        in_specs=left_specs + [vmem] * 4,
+        out_specs=[vmem, vmem, vmem],
         out_shape=[
             jax.ShapeDtypeStruct((tokens, width), BF16),
             jax.ShapeDtypeStruct(small, BF16),
+            jax.ShapeDtypeStruct((16, width) if way == "norm" else (16, 128), BF16),
         ],
         scratch_shapes=[
             pltpu.VMEM((tokens, width), BF16),
-            pltpu.VMEM((2, places, rows, width // 2), BF16),
-            pltpu.VMEM((2, places - 1, rows, width // 2), BF16),
-            pltpu.SemaphoreType.DMA((2, places - 1)),
-            pltpu.SemaphoreType.DMA((2, places - 1)),
-            pltpu.SemaphoreType.DMA((2, bits, places)),
-            pltpu.SemaphoreType.DMA((2, places)),
+            pltpu.VMEM((parts, places, rows, width // parts), BF16),
+            pltpu.VMEM((parts, places - 1, rows, width // parts), BF16),
+            pltpu.SemaphoreType.DMA((parts, places - 1)),
+            pltpu.SemaphoreType.DMA((parts, places - 1)),
+            pltpu.SemaphoreType.DMA((parts, bits, places)),
+            pltpu.SemaphoreType.DMA((parts, places)),
+            pltpu.SemaphoreType.DMA((2,)),
         ],
         compiler_params=pltpu.CompilerParams(
             collective_id=number, has_side_effects=True, vmem_limit_bytes=56 * 1024 * 1024
         ),
         name="summed_" + way,
-    )(left, right, rest, gain.reshape(1, -1), bias.reshape(1, -1))
+    )(*lefts, right, rest, gain.reshape(1, -1), bias.reshape(1, -1))
 
 
 def own_rows(matrix):
@@ -539,7 +585,9 @@
     normed = layer_norm(stream, time_norm_gain, time_norm_bias)
     ctx_place = lax.axis_index("ctx")
     ctx_first = ctx_place == 0
-    arrived = passed_along(normed[-1:], "ctx", 1)
+    arrived = passed_along(
+        layer_norm(lax.optimization_barrier(stream[-1:]), time_norm_gain, time_norm_bias), "ctx", 1
+    )
     previous = jnp.concatenate(
         [jnp.where(ctx_first, time_previous_token[None, :], arrived), normed[:-1]], axis=0
     )
@@ -566,26 +614,35 @@
             head_group_bias,
         ]
     )
-    zero, reader, extra, moved = wkv_local(
-        recept, keys, values, decay_low, rate_low, decay_second_factor, rate_second_factor, vec
-    )
-    arrivals = [passed_along(moved, "ctx", by) for by in range(1, lax.axis_size("ctx"))]
-    lagged_embedding = wkv_finish(
-        ctx_place.reshape(1).astype(jnp.int32),
-        zero,
-        reader,
-        extra,
-        gate_low,
-        gate_second_factor,
-        vec,
-        head_state_initial,
-        arrivals,
-    )
-    normed_next, middle = summed(
+    locals_ = [
+        wkv_local(
+            half, recept, keys, values, decay_low, rate_low,
+            decay_second_factor, rate_second_factor, vec,
+        )
+        for half in range(2)
+    ]
+    arrivals = [
+        [passed_along(parts[3], "ctx", by) for by in range(1, lax.axis_size("ctx"))]
+        for parts in locals_
+    ]
+    lagged_embedding = [
+        wkv_finish(
+            half,
+            ctx_place.reshape(1).astype(jnp.int32),
+            *locals_[half][:3],
+            gate_low,
+            gate_second_factor,
+            vec,
+            head_state_initial,
+            arrivals[half],
+        )
+        for half in range(2)
+    ]
+    normed_next, middle, last_rows = summed(
         "norm", 0, lagged_embedding, time_output_weight, own_rows(stream),
         channel_norm_gain, channel_norm_bias,
     )
-    arrived_next = passed_along(normed_next[-1:], "ctx", 1)
+    arrived_next = last_rows[-1:]
     previous_next = jnp.concatenate(
         [jnp.where(ctx_first, channel_previous_token[None, :], arrived_next), normed_next[:-1]],
         axis=0,
@@ -595,8 +652,8 @@
         jnp.dot(channel_in, channel_key_weight, preferred_element_type=jnp.float32), 0.0
     )
     hidden = (expanded * expanded).astype(jnp.bfloat16)
-    layer_out, _ = summed(
-        "plain", 1, hidden, channel_value_weight, middle, channel_norm_gain, channel_norm_bias
+    layer_out, _, _ = summed(
+        "plain", 1, [hidden], channel_value_weight, middle, channel_norm_gain, channel_norm_bias
     )
     return layer_out
 

time: 206 us -> 203 us (0.985)
  starting transfers between devices: 20.4 us -> 16 us
  other arithmetic: 6.63 us -> 10.8 us
    ppermute x5 -> x7, starting transfers between devices: 20.4 us -> 16 us  [passed_along(): return lax.ppermute(shard, axis, pairs)]
    convert_element_type x1 -> x2, other arithmetic: 2.31 us -> 4.49 us  [layer_norm(): (centered * lax.rsqrt(variance + 1e-05) * gain_vec + bias_vec).astype(jnp...]
    pallas_call x3 -> x4, Pallas kernels: 128 us -> 128 us  [the longest x2 108 us: summed(): pl.pallas_call(functools.partial(summed_kernel, way, places, len(left)),...]
    pallas_call x1 -> x2, Pallas kernels: 4.89 us -> 4.81 us  [wkv_finish(): pl.pallas_call(finish_kernel, grid=(count,), in_specs=[pl.BlockSpec(memor...]
  transfers between devices with their start and end apart: 5 -> 7, of which waited for: 2 -> 0; matrix products, arithmetic and copies ran while one was open for 2% -> 6% of each run, Pallas kernels for 0% -> 6%
where the time goes in v3:
time: 203 us; the launch traced here: 202 us
  Pallas kernels  133 us (66%)
  matrix products  30.7 us (15%)
  starting transfers between devices  16 us (8%)
  other arithmetic  10.8 us (5%)
  local copies, waits for them, and re-layouts  9.33 us (5%)
    pallas_call x2, Pallas kernels, summed(): pl.pallas_call(functools.partial(summed_kernel, way, places, len(left)),...  108 us
    pallas_call x2, Pallas kernels, wkv_local(): pl.pallas_call(local_kernel, grid=(count,), in_specs=[picked, picked, pic...  20.2 us
    ppermute x7, starting transfers between devices, passed_along(): return lax.ppermute(shard, axis, pairs)  16 us
    dot_general x1, matrix products, shards(): jnp.dot(channel_in, channel_key_weight, preferred_element_type=jnp.float32)  11.4 us
    unnamed x57, local copies, waits for them, and re-layouts  6.4 us
    dot_general x1, matrix products, shards(): jnp.dot(inputs[4], rate_first_factor, preferred_element_type=F32)  5.8 us
    pallas_call x2, Pallas kernels, wkv_finish(): pl.pallas_call(finish_kernel, grid=(count,), in_specs=[pl.BlockSpec(memor...  4.81 us
    convert_element_type x2, other arithmetic, layer_norm(): (centered * lax.rsqrt(variance + 1e-05) * gain_vec + bias_vec).astype(jnp...  4.49 us
  transfers between devices with their start and end apart: 7, of which 0 were waited for; matrix products, arithmetic and copies ran while one was open for 6% of the time, Pallas kernels for 6%

profile of v3, /device:TPU:0, one launch (start us, length us, event | category | flops | bytes accessed | tf_op | source)
XLA Modules:
  0.0 202.2 jit_solution(14948513900551867148)
XLA Ops:
  4.6 5.1 %collective-permute-start = (bf16[1,4096]{1,0:T(2,128)(2,1)S(1)}, bf16[1,4096]{1,0:T(2,128)(2,1)S(1)}, u32[]{:S(2)}, u32[]{:S(2)}) collective-permute-start(bf16[1,4096]{1,0:T(2,128)(2,1)S(1)} %add_convert_fusion), channel_id=1, source_target_pairs={{0,8},{8,16},{16,24},{1,9},{9,17},{17,25},{2,10},{10,18},{18,26},{... | collective-permute-start | bytes 24584 | tf_op jit(solution)/shard_map/ppermute | solution.py:20
  9.7 2.8 %convert_reduce_fusion = f32[512]{0:T(512)S(1)} fusion(bf16[512,4096]{1,0:T(8,128)(2,1)} %param.29), kind=kLoop, calls=%fused_computation.10 | loop fusion | flops 4193792 | bytes 4196352 | tf_op jit(solution)/shard_map/reduce_sum | solution.py:25
  13.9 3.6 %fusion.5 = bf16[512,4096]{1,0:T(8,128)(2,1)} fusion(bf16[512,4096]{1,0:T(8,128)(2,1)S(1)} %copy-done.8, f32[4096]{0:T(1024)S(1)} %copy-done.11, f32[4096]{0:T(1024)S(1)} %copy-done.12, f32[512]{0:T(512)S(1)} %add_rsqrt_fusion, f32[512]{0:T(512)S(1)} %broadcast_multiply_fusion), kind=kLoop, calls=%fused_computation.16 | loop fusion | flops 12582912 | bytes 8425472 | tf_op jit(solution)/shard_map/convert_element_type | solution.py:28
  17.8 5.8 %fusion.68.rlow_ref = bf16[512,128]{1,0:T(8,128)(2,1)S(1)} fusion(bf16[4096,128]{1,0:T(8,128)(2,1)S(1)} %copy-done.26, bf16[512,4096]{1,0:T(8,128)(2,1)} %fusion.5, f32[4096]{0:T(1024)S(1)} %bitcast.44, bf16[511,4096]{1,0:T(8,128)(2,1)} %bitcast.27, bf16[1,4096]{1,0:T(2,128)(2,1)S(1)} %broadcast_select_fusion.1), kind=kOutput, calls=%fused_computation.52 | convolution fusion | flops 555810816 | bytes 9584640 | tf_op jit(solution)/shard_map/dot_general | solution.py:601
  23.6 3.2 %fusion.65.dlow_ref = bf16[512,128]{1,0:T(8,128)(2,1)S(1)} fusion(bf16[4096,128]{1,0:T(8,128)(2,1)S(1)} %copy-done.27, bf16[512,4096]{1,0:T(8,128)(2,1)S(1)} %copy-done.9, f32[4096]{0:T(1024)S(1)} %bitcast.43, bf16[511,4096]{1,0:T(8,128)(2,1)S(1)} %bitcast.28, bf16[1,4096]{1,0:T(2,128)(2,1)S(1)} %broadcast_select_fusion.1), kind=kOutput, calls=%fused_computation.51 | convolution fusion | flops 555810816 | bytes 9584640 | tf_op jit(solution)/shard_map/dot_general | solution.py:599
  26.9 2.3 %fusion.44.value_ref = bf16[512,512]{1,0:T(8,128)(2,1)S(1)} fusion(bf16[4096,512]{1,0:T(8,128)(2,1)S(1)} %copy-done.23, bf16[512,4096]{1,0:T(8,128)(2,1)S(1)} %copy-done.9, f32[4096]{0:T(1024)S(1)} %bitcast.42, bf16[511,4096]{1,0:T(8,128)(2,1)S(1)} %bitcast.29, bf16[1,4096]{1,0:T(2,128)(2,1)S(1)} %broadcast_select_fusion.1), kind=kOutput, calls=%fused_computation.44 | convolution fusion | flops 2166620160 | bytes 13123584 | tf_op jit(solution)/shard_map/dot_general | solution.py:597
  29.2 2.5 %fusion.41.key_ref = bf16[512,512]{1,0:T(8,128)(2,1)S(1)} fusion(bf16[4096,512]{1,0:T(8,128)(2,1)S(1)} %copy-done.24, bf16[512,4096]{1,0:T(8,128)(2,1)S(1)} %copy-done.9, f32[4096]{0:T(1024)S(1)} %bitcast.41, bf16[511,4096]{1,0:T(8,128)(2,1)S(1)} %bitcast.30, bf16[1,4096]{1,0:T(2,128)(2,1)S(1)} %broadcast_select_fusion.1), kind=kOutput, calls=%fused_computation.43 | convolution fusion | flops 2166620160 | bytes 13123584 | tf_op jit(solution)/shard_map/dot_general | solution.py:596
  31.8 2.4 %fusion.38.recept_ref = bf16[512,512]{1,0:T(8,128)(2,1)S(1)} fusion(bf16[4096,512]{1,0:T(8,128)(2,1)S(1)} %copy-done.25, bf16[512,4096]{1,0:T(8,128)(2,1)S(1)} %copy-done.9, f32[4096]{0:T(1024)S(1)} %bitcast.40, bf16[511,4096]{1,0:T(8,128)(2,1)S(1)} %bitcast.31, bf16[1,4096]{1,0:T(2,128)(2,1)S(1)} %broadcast_select_fusion.1), kind=kOutput, calls=%fused_computation.42 | convolution fusion | flops 2166620160 | bytes 13123584 | tf_op jit(solution)/shard_map/dot_general | solution.py:595
  34.2 10.1 %wkv_local.3 = (f32[512,256]{1,0:T(8,128)S(1)}, bf16[512,256]{1,0:T(8,128)(2,1)S(1)}, f32[512,256]{1,0:T(8,128)S(1)}, bf16[2,2,64,128]{3,2,1,0:T(8,128)(2,1)S(1)}) custom-call(bf16[512,512]{1,0:T(8,128)(2,1)S(1)} %fusion.38.recept_ref, bf16[512,512]{1,0:T(8,128)(2,1)S(1)} %fusion.41.key_ref, bf16[512,512]{1,0:T(8,128)(2,1)S(1)} %fusion.44.value_ref, ...), custom_call_target="tpu_custom_call" | custom-call | flops 536870912 | bytes 2621440 | tf_op jit(solution)/shard_map/wkv_local/pallas_call | solution.py:219
  44.3 3.3 %collective-permute-start.6 = (bf16[2,2,64,128]{3,2,1,0:T(8,128)(2,1)S(1)}, bf16[2,2,64,128]{3,2,1,0:T(8,128)(2,1)S(1)}, u32[]{:S(2)}, u32[]{:S(2)}) collective-permute-start(bf16[2,2,64,128]{3,2,1,0:T(8,128)(2,1)S(1)} %get-tuple-element.24), channel_id=1, source_target_pairs={{0,24},{1,25},{2,26},{3,27},{4,28},{5,29},{6,30},{7,31}} | collective-permute-start | bytes 196616 | tf_op jit(solution)/shard_map/ppermute | solution.py:20
  47.7 1.9 constant_dynamic-slice_fusion.refs_3_
  49.5 1.8 collective-permute-start.5
  51.4 1.9 collective-permute-start.4
  53.3 10.1 %wkv_local.2 = (f32[512,256]{1,0:T(8,128)S(1)}, bf16[512,256]{1,0:T(8,128)(2,1)S(1)}, f32[512,256]{1,0:T(8,128)S(1)}, bf16[2,2,64,128]{3,2,1,0:T(8,128)(2,1)S(1)}) custom-call(bf16[512,512]{1,0:T(8,128)(2,1)S(1)} %fusion.38.recept_ref, bf16[512,512]{1,0:T(8,128)(2,1)S(1)} %fusion.41.key_ref, bf16[512,512]{1,0:T(8,128)(2,1)S(1)} %fusion.44.value_ref, ...), custom_call_target="tpu_custom_call" | custom-call | flops 536870912 | bytes 2621440 | tf_op jit(solution)/shard_map/wkv_local/pallas_call | solution.py:219
  63.4 1.3 collective-permute-start.3
  64.7 1.3 collective-permute-start.2
  66.0 1.3 collective-permute-start.1
  67.3 3.0 %fusion.59.glow_ref = bf16[512,256]{1,0:T(8,128)(2,1)S(1)} fusion(bf16[4096,256]{1,0:T(8,128)(2,1)S(1)} %copy-done, bf16[512,4096]{1,0:T(8,128)(2,1)S(1)} %copy-done.9, f32[4096]{0:T(1024)S(1)} %bitcast.39, bf16[511,4096]{1,0:T(8,128)(2,1)S(1)} %bitcast.32, bf16[1,4096]{1,0:T(2,128)(2,1)S(1)} %broadcast_select_fusion.1), kind=kOutput, calls=%fused_computation.49 | convolution fusion | flops 1093140480 | bytes 10764288 | tf_op jit(solution)/shard_map/dot_general | solution.py:603
  70.4 2.4 %wkv_finish.3.refs_1_ = bf16[512,256]{1,0:T(8,128)(2,1)S(1)} custom-call(s32[1]{0:T(128)} %bitcast.place_ref, f32[512,256]{1,0:T(8,128)S(1)} %get-tuple-element.21.zero_ref, bf16[512,256]{1,0:T(8,128)(2,1)S(1)} %get-tuple-element.22.reader_ref, f32[512,256]{1,0:T(8,128)S(1)} %get-tuple-element.23.extra_ref, bf16[512,256]{1,0:T(8,128)(2,1)S(1)} %fusion.59.glow_ref, ...), custom_call_target="tpu_custom_call" | custom-call | flops 134217728 | bytes 1835008 | tf_op jit(solution)/shard_map/wkv_finish/pallas_call | solution.py:279
  73.6 2.4 %wkv_finish.2.refs_0_ = bf16[512,256]{1,0:T(8,128)(2,1)S(1)} custom-call(s32[1]{0:T(128)} %bitcast.place_ref, f32[512,256]{1,0:T(8,128)S(1)} %get-tuple-element.17.zero_ref, bf16[512,256]{1,0:T(8,128)(2,1)S(1)} %get-tuple-element.18.reader_ref, f32[512,256]{1,0:T(8,128)S(1)} %get-tuple-element.19.extra_ref, bf16[512,256]{1,0:T(8,128)(2,1)S(1)} %fusion.59.glow_ref, ...), custom_call_target="tpu_custom_call" | custom-call | flops 134217728 | bytes 1835008 | tf_op jit(solution)/shard_map/wkv_finish/pallas_call | solution.py:279
  76.7 55.4 %summed_norm.1 = (bf16[512,4096]{1,0:T(8,128)(2,1)}, bf16[64,4096]{1,0:T(8,128)(2,1)}, bf16[16,4096]{1,0:T(8,128)(2,1)}) custom-call(bf16[512,256]{1,0:T(8,128)(2,1)} %copy-done.3, bf16[512,256]{1,0:T(8,128)(2,1)} %copy-done.2, bf16[512,4096]{1,0:T(8,128)(2,1)} %refs_2_.1, bf16[64,4096]{1,0:T(8,128)(2,1)} %constant_dynamic-slice_fusion.refs_3_, ...), custom_call_target="tpu_custom_call" | custom-call | tf_op jit(solution)/shard_map/summed_norm/pallas_call | solution.py:519
  133.0 11.4 %multiply_convert_fusion.refs_0_ = bf16[512,1024]{1,0:T(8,128)(2,1)} fusion(bf16[4096,1024]{1,0:T(8,128)(2,1)} %param.56, bf16[512,4096]{1,0:T(8,128)(2,1)} %get-tuple-element.25, bf16[511,4096]{1,0:T(8,128)(2,1)} %bitcast.53, bf16[1,4096]{1,0:T(2,128)(2,1)S(1)} %broadcast_select_fusion, f32[4096]{0:T(1024)S(1)} %convert_element_type.111), kind=kOutput, calls=%fused_computation.41 | convolution fusion | flops 4315414528 | bytes 17842176 | tf_op jit(solution)/shard_map/dot_general | solution.py:652
  144.4 52.9 %summed_plain.1 = (bf16[512,4096]{1,0:T(8,128)(2,1)}, bf16[8,128]{1,0:T(8,128)(2,1)}, bf16[16,128]{1,0:T(8,128)(2,1)}) custom-call(bf16[512,1024]{1,0:T(8,128)(2,1)} %multiply_convert_fusion.refs_0_, bf16[1024,4096]{1,0:T(8,128)(2,1)} %refs_1_.1, bf16[64,4096]{1,0:T(8,128)(2,1)} %get-tuple-element.27.refs_2_, f32[1,4096]{1,0:T(1,128)} %bitcast.34, ...), custom_call_target="tpu_custom_call" | custom-call | tf_op jit(solution)/shard_map/summed_plain/pallas_call | solution.py:519
  197.3 4.8 %copy.31 = bf16[512,4096]{1,0:T(8,128)(2,1)} copy(bf16[512,4096]{1,0:T(8,128)(2,1)} %get-tuple-element.28) | data formatting | bytes 8388608
  (75 shorter events, 7.0 us)
Async XLA Ops:
  0.0 67.3 %copy-start = (bf16[4096,256]{1,0:T(8,128)(2,1)S(1)}, bf16[4096,256]{1,0:T(8,128)(2,1)}, u32[]{:S(2)}) copy-start(bf16[4096,256]{1,0:T(8,128)(2,1)} %param.45) | copy-start | bytes 6291460
  3.6 8.9 %copy-start.8 = (bf16[512,4096]{1,0:T(8,128)(2,1)S(1)}, bf16[512,4096]{1,0:T(8,128)(2,1)}, u32[]{:S(2)}) copy-start(bf16[512,4096]{1,0:T(8,128)(2,1)} %param.29) | copy-start | bytes 12582916
  4.6 9.2 %copy-start.11 = (f32[4096]{0:T(1024)S(1)}, f32[4096]{0:T(1024)}, u32[]{:S(2)}) copy-start(f32[4096]{0:T(1024)} %param.34) | copy-start | bytes 49156
  4.6 9.2 %copy-start.12 = (f32[4096]{0:T(1024)S(1)}, f32[4096]{0:T(1024)}, u32[]{:S(2)}) copy-start(f32[4096]{0:T(1024)} %param.33) | copy-start | bytes 49156
  4.6 13.1 %collective-permute-start = (bf16[1,4096]{1,0:T(2,128)(2,1)S(1)}, bf16[1,4096]{1,0:T(2,128)(2,1)S(1)}, u32[]{:S(2)}, u32[]{:S(2)}) collective-permute-start(bf16[1,4096]{1,0:T(2,128)(2,1)S(1)} %add_convert_fusion), channel_id=1, source_target_pairs={{0,8},{8,16},{16,24},{1,9},{9,17},{17,25},{2,10},{10,18},{18,26},{... | collective-permute-start | bytes 24584 | tf_op jit(solution)/shard_map/ppermute | solution.py:20
  13.8 3.8 %copy-start.14 = (f32[512]{0:T(512)S(1)}, f32[512]{0:T(512)}, u32[]{:S(2)}) copy-start(f32[512]{0:T(512)} %param.51) | copy-start | bytes 6148
  13.8 3.8 %copy-start.17 = (f32[512]{0:T(512)S(1)}, f32[512]{0:T(512)}, u32[]{:S(2)}) copy-start(f32[512]{0:T(512)} %param.41) | copy-start | bytes 6148
  13.8 3.8 %copy-start.18 = (f32[512]{0:T(512)S(1)}, f32[512]{0:T(512)}, u32[]{:S(2)}) copy-start(f32[512]{0:T(512)} %param.44) | copy-start | bytes 6148
  13.8 3.8 %copy-start.19 = (f32[512]{0:T(512)S(1)}, f32[512]{0:T(512)}, u32[]{:S(2)}) copy-start(f32[512]{0:T(512)} %param.47) | copy-start | bytes 6148
  13.8 3.8 %copy-start.20 = (f32[512]{0:T(512)S(1)}, f32[512]{0:T(512)}, u32[]{:S(2)}) copy-start(f32[512]{0:T(512)} %param.48) | copy-start | bytes 6148
  13.8 3.8 %copy-start.21 = (f32[512]{0:T(512)S(1)}, f32[512]{0:T(512)}, u32[]{:S(2)}) copy-start(f32[512]{0:T(512)} %param.49) | copy-start | bytes 6148
  13.9 3.9 %copy-start.15 = (bf16[4096]{0:T(1024)(128)(2,1)S(1)}, bf16[4096]{0:T(1024)(128)(2,1)}, u32[]{:S(2)}) copy-start(bf16[4096]{0:T(1024)(128)(2,1)} %param.30) | copy-start | bytes 24580
  13.9 3.9 %copy-start.26 = (bf16[4096,128]{1,0:T(8,128)(2,1)S(1)}, bf16[4096,128]{1,0:T(8,128)(2,1)}, u32[]{:S(2)}) copy-start(bf16[4096,128]{1,0:T(8,128)(2,1)} %param.42) | copy-start | bytes 3145732
  17.8 5.8 %copy-start.9 = (bf16[512,4096]{1,0:T(8,128)(2,1)S(1)}, bf16[512,4096]{1,0:T(8,128)(2,1)}, u32[]{:S(2)}) copy-start(bf16[512,4096]{1,0:T(8,128)(2,1)} %fusion.5) | copy-start | bytes 12582916
  17.8 5.8 %copy-start.27 = (bf16[4096,128]{1,0:T(8,128)(2,1)S(1)}, bf16[4096,128]{1,0:T(8,128)(2,1)}, u32[]{:S(2)}) copy-start(bf16[4096,128]{1,0:T(8,128)(2,1)} %param.39) | copy-start | bytes 3145732
  31.7 17.8 %copy-start.13 = (bf16[4096]{0:T(1024)(128)(2,1)S(1)}, bf16[4096]{0:T(1024)(128)(2,1)}, u32[]{:S(2)}) copy-start(bf16[4096]{0:T(1024)(128)(2,1)} %param.55) | copy-start | bytes 24580
  44.3 21.7 %collective-permute-start.6 = (bf16[2,2,64,128]{3,2,1,0:T(8,128)(2,1)S(1)}, bf16[2,2,64,128]{3,2,1,0:T(8,128)(2,1)S(1)}, u32[]{:S(2)}, u32[]{:S(2)}) collective-permute-start(bf16[2,2,64,128]{3,2,1,0:T(8,128)(2,1)S(1)} %get-tuple-element.24), channel_id=1, source_target_pairs={{0,24},{1,25},{2,26},{3,27},{4,28},{5,29},{6,30},{7,31}} | collective-permute-start | bytes 196616 | tf_op jit(solution)/shard_map/ppermute | solution.py:20
  49.5 20.9 %collective-permute-start.5 = (bf16[2,2,64,128]{3,2,1,0:T(8,128)(2,1)S(1)}, bf16[2,2,64,128]{3,2,1,0:T(8,128)(2,1)S(1)}, u32[]{:S(2)}, u32[]{:S(2)}) collective-permute-start(bf16[2,2,64,128]{3,2,1,0:T(8,128)(2,1)S(1)} %get-tuple-element.24), channel_id=1, source_target_pairs={{0,16},{8,24},{1,17},{9,25},{2,18},{10,26},{3,19},{11,27},{4,20},{... | collective-permute-start | bytes 196616 | tf_op jit(solution)/shard_map/ppermute | solution.py:20
  51.4 19.0 %collective-permute-start.4 = (bf16[2,2,64,128]{3,2,1,0:T(8,128)(2,1)S(1)}, bf16[2,2,64,128]{3,2,1,0:T(8,128)(2,1)S(1)}, u32[]{:S(2)}, u32[]{:S(2)}) collective-permute-start(bf16[2,2,64,128]{3,2,1,0:T(8,128)(2,1)S(1)} %get-tuple-element.24), channel_id=1, source_target_pairs={{0,8},{8,16},{16,24},{1,9},{9,17},{17,25},{2,10},{10,18},{18,26},{... | collective-permute-start | bytes 196616 | tf_op jit(solution)/shard_map/ppermute | solution.py:20
  63.4 10.2 %collective-permute-start.3 = (bf16[2,2,64,128]{3,2,1,0:T(8,128)(2,1)S(1)}, bf16[2,2,64,128]{3,2,1,0:T(8,128)(2,1)S(1)}, u32[]{:S(2)}, u32[]{:S(2)}) collective-permute-start(bf16[2,2,64,128]{3,2,1,0:T(8,128)(2,1)S(1)} %get-tuple-element.20), channel_id=1, source_target_pairs={{0,24},{1,25},{2,26},{3,27},{4,28},{5,29},{6,30},{7,31}} | collective-permute-start | bytes 196616 | tf_op jit(solution)/shard_map/ppermute | solution.py:20
  64.7 8.9 %collective-permute-start.2 = (bf16[2,2,64,128]{3,2,1,0:T(8,128)(2,1)S(1)}, bf16[2,2,64,128]{3,2,1,0:T(8,128)(2,1)S(1)}, u32[]{:S(2)}, u32[]{:S(2)}) collective-permute-start(bf16[2,2,64,128]{3,2,1,0:T(8,128)(2,1)S(1)} %get-tuple-element.20), channel_id=1, source_target_pairs={{0,16},{8,24},{1,17},{9,25},{2,18},{10,26},{3,19},{11,27},{4,20},{... | collective-permute-start | bytes 196616 | tf_op jit(solution)/shard_map/ppermute | solution.py:20
  66.0 7.6 %collective-permute-start.1 = (bf16[2,2,64,128]{3,2,1,0:T(8,128)(2,1)S(1)}, bf16[2,2,64,128]{3,2,1,0:T(8,128)(2,1)S(1)}, u32[]{:S(2)}, u32[]{:S(2)}) collective-permute-start(bf16[2,2,64,128]{3,2,1,0:T(8,128)(2,1)S(1)} %get-tuple-element.20), channel_id=1, source_target_pairs={{0,8},{8,16},{16,24},{1,9},{9,17},{17,25},{2,10},{10,18},{18,26},{... | collective-permute-start | bytes 196616 | tf_op jit(solution)/shard_map/ppermute | solution.py:20
  73.5 58.6 %copy-start.16 = (bf16[4096]{0:T(1024)(128)(2,1)S(1)}, bf16[4096]{0:T(1024)(128)(2,1)}, u32[]{:S(2)}) copy-start(bf16[4096]{0:T(1024)(128)(2,1)} %param.31) | copy-start | bytes 24580
  197.3 4.9 %copy-start.1 = (bf16[4096,256]{1,0:T(8,128)(2,1)S(1)}, bf16[4096,256]{1,0:T(8,128)(2,1)}, u32[]{:S(2)}) copy-start(bf16[4096,256]{1,0:T(8,128)(2,1)} %param.45) | copy-start | bytes 6291460
  (11 other events, 28.1 us)
